TPU v7x, 32 devices: a whole 2x2x4 slice. The times are simulated.
32 devices in a mesh: grp: 2 (over y), ctx: 4 (over z), head: 2 (over x), sub: 2 (over core).
Axes of the slice: x: 2, y: 2, z: 4, core: 2. Of those that a mesh axis runs over, the one named last changes fastest.
Arguments:
- queries: bfloat16 [512, 16384], P(('grp', 'ctx', 'head', 'sub')), parts along dimension 0, may hold values from -400 to 400
- kv_cache: bfloat16 [2, 8192, 1024], P(None, ('grp', 'ctx', 'sub'), 'head'), parts along dimension 1, may hold values from -6 to 6
- page_counts: int32 [8], P('grp'), parts along dimension 0, may hold values from 1 to 4, as said below
Outputs:
- attended: bfloat16 [512, 16384], P(('grp', 'ctx', 'head', 'sub')), parts along dimension 0
There are 2 independent parts, one for each index of `grp`. A program takes and returns all parts, laid end to end along the dimension named above; each array names one. Nothing has to cross between parts.
Inputs may be any that keep to these rules, and one draw needn't show every extreme that they name: `page_counts`: each count is at least 1, the counts sum to exactly 8, and one request has exactly 4 pages.
All inputs are finite; a program needn't handle non-finite values.
Results may differ from a plain program's by a relative error of at most 0.014.
Values may be sent and summed in bfloat16 or wider, within the bound.
A program may use at most 64 MiB of HBM per device.

v0:
```python
import functools
import math

import jax
import jax.numpy as jnp
from jax import lax
from jax.experimental import pallas as pl
from jax.experimental.pallas import tpu as pltpu
from jax.sharding import PartitionSpec as P

HQ = 128
KVH = 8
HD = 128
REQS = 4
QR = 64
PAGE = 256
SPAN = 256


NEG = -1e30
MESH = pl.DeviceIdType.MESH
ROW_BLOCK = 256


def from_behind(array, axis, by):
    count = lax.axis_size(axis)
    pairs = [(i, i + by) for i in range(count) if 0 <= i + by < count]
    return lax.ppermute(array, axis, pairs)


def per_device(queries, kv_cache, page_counts):
    per_group = HQ // KVH
    local_heads = kv_cache.shape[2] // HD
    ctx_size = lax.axis_size("ctx")
    sub_size = lax.axis_size("sub")
    head_count = lax.axis_size("head")
    tok_rows = queries.shape[0]
    score_scale = HD ** (-0.5)
    regrouped = lax.all_to_all(queries, "head", split_axis=1, concat_axis=0, tiled=True)
    all_queries = lax.all_gather(regrouped, ("ctx", "sub"), axis=0, tiled=True)
    all_queries = all_queries.reshape(SPAN, local_heads, per_group, HD)
    page_ends = jnp.cumsum(page_counts)
    ctx_rows = SPAN // ctx_size
    offsets = jnp.arange(QR, dtype=jnp.int32)
    columns = jnp.arange(PAGE, dtype=jnp.int32)
    flat_index = lax.axis_index("ctx") * sub_size + lax.axis_index("sub")
    pages_here = kv_cache.shape[1] // PAGE
    base_pages = pages_here * ctx_size * sub_size // 2
    initial = (
        jnp.full((SPAN, local_heads, per_group), NEG, jnp.float32),
        jnp.zeros((SPAN, local_heads, per_group), jnp.float32),
        jnp.zeros((SPAN, local_heads, per_group, HD), jnp.float32),
    )
    half_rows = kv_cache.shape[1] // 2
    arrived = from_behind(kv_cache[:, half_rows:], "ctx", -(ctx_size // 2))
    is_lower = lax.axis_index("ctx") < ctx_size // 2
    source_flat = flat_index + ctx_size // 2 * sub_size
    working = jnp.where(is_lower, arrived, kv_cache[:, :half_rows])
    first_page = jnp.where(
        is_lower, source_flat * pages_here + pages_here // 2, flat_index * pages_here
    )
    page_total = working.shape[1] // PAGE

    def add_page(page_turn, running):
        page_index = first_page + page_turn
        relative = page_index - base_pages
        counted = jnp.sum((relative >= page_ends).astype(jnp.int32))
        request = jnp.where(relative < 0, REQS, counted)

        def update(partial_value):
            run_max, run_sum, run_out = partial_value
            request_id = jnp.minimum(request, REQS - 1)
            row_start = request_id * QR
            gathered = row_start + offsets
            within = gathered % ctx_rows
            ctx_block = gathered // ctx_rows
            sub_part = within // (head_count * tok_rows)
            head_part = within // tok_rows % head_count
            tok_part = within % tok_rows
            natural = ctx_block * ctx_rows + (head_part * sub_size + sub_part) * tok_rows + tok_part
            query_pos = (page_ends[request_id] + base_pages) * PAGE - QR + natural - row_start
            key_pos = page_index * PAGE + columns
            visible = key_pos[None, :] <= query_pos[:, None]
            page_keys = working[0].reshape(PAGE, local_heads, HD)
            page_values = working[1].reshape(PAGE, local_heads, HD)
            query_rows = lax.dynamic_slice_in_dim(all_queries, row_start, QR, 0)
            scores = (
                jnp.einsum(
                    "qkgd,pkd->qkgp", query_rows, page_keys, preferred_element_type=jnp.float32
                )
                * score_scale
            )
            scores = jnp.where(visible[:, None, None, :], scores, NEG)
            old_max = lax.dynamic_slice_in_dim(run_max, row_start, QR, 0)
            old_sum = lax.dynamic_slice_in_dim(run_sum, row_start, QR, 0)
            old_out = lax.dynamic_slice_in_dim(run_out, row_start, QR, 0)
            new_max = jnp.maximum(old_max, jnp.max(scores, axis=3))
            factor = jnp.exp(old_max - new_max)
            numerators = jnp.exp(scores - new_max[..., None])
            new_sum = old_sum * factor + jnp.sum(numerators, axis=3)
            product = jnp.einsum(
                "qkgp,pkd->qkgd",
                numerators.astype(jnp.bfloat16),
                page_values,
                preferred_element_type=jnp.float32,
            )
            new_out = old_out * factor[..., None] + product
            return (
                lax.dynamic_update_slice_in_dim(run_max, new_max, row_start, 0),
                lax.dynamic_update_slice_in_dim(run_sum, new_sum, row_start, 0),
                lax.dynamic_update_slice_in_dim(run_out, new_out, row_start, 0),
            )

        def unchanged(partial_value):
            return partial_value

        return lax.cond(request < REQS, update, unchanged, running)

    run_max, run_sum, run_out = lax.fori_loop(0, page_total, add_page, initial)
    share = SPAN // (ctx_size * sub_size)
    global_max = lax.pmax(run_max, ("ctx", "sub"))
    factor = jnp.exp(run_max - global_max)
    sums_here, outs_here = (
        lax.psum_scatter(
            (run_sum * factor).astype(jnp.bfloat16), ("ctx", "sub"), scatter_dimension=0, tiled=True
        ).astype(jnp.float32),
        lax.psum_scatter(
            (run_out * factor[..., None]).astype(jnp.bfloat16),
            ("ctx", "sub"),
            scatter_dimension=0,
            tiled=True,
        ).astype(jnp.float32),
    )
    finished = (outs_here / sums_here[..., None]).astype(jnp.bfloat16)
    finished = finished.reshape(share, local_heads * per_group * HD)
    return lax.all_to_all(finished, "head", split_axis=0, concat_axis=1, tiled=True)


def page_plan(ctx_size, sub_size, pages_here):
    live = pages_here * ctx_size * sub_size // 2
    base = live
    last = ctx_size - 1
    low = [0 if r == 0 else live // 2 if r == last else r for r in range(ctx_size)]
    high = [live // 2 if r == 0 else live if r == last else live - (last - r) for r in range(ctx_size)]
    plane_of = [(base + p) // (pages_here * sub_size) for p in range(live)]
    core_of = [(base + p) // pages_here % sub_size for p in range(live)]
    return live, low, high, plane_of, core_of


def can_ship(mesh, rows):
    ctx_size, sub_size, head_size = mesh.shape["ctx"], mesh.shape["sub"], mesh.shape["head"]
    if ctx_size != REQS or SPAN // ctx_size != QR:
        return False
    pages_here = rows // (mesh.shape["grp"] * ctx_size * sub_size) // PAGE
    if pages_here < 1 or KVH % (head_size * sub_size):
        return False
    live, low, high, plane_of, _ = page_plan(ctx_size, sub_size, pages_here)
    ahead = any(
        low[r] <= p < high[r] and r > plane_of[p] for r in range(ctx_size) for p in range(live)
    )
    return not ahead


def ship_kernel(
    sizes,
    counts_ref,
    q_hbm,
    kv_hbm,
    out_hbm,
    kvbuf,
    qbuf,
    qs,
    sbuf,
    mx,
    lsum,
    acc,
    obuf,
    q_send,
    q_recv,
    o_send,
    o_recv,
    kv_send,
    kv_recv,
    relay_send,
):
    ctx_size, sub_size, head_size, pages_here, local_heads = sizes
    live, low, high, plane_of, core_of = page_plan(ctx_size, sub_size, pages_here)
    hub = plane_of[0]
    per_core = local_heads // sub_size
    moved = per_core - per_core // 2
    group = HQ // KVH
    width = group * HD
    plane_devices = head_size * sub_size
    tok_rows = QR // plane_devices
    z, x, s = lax.axis_index("ctx"), lax.axis_index("head"), lax.axis_index("sub")
    mine = x * sub_size + s
    rows = QR * group

    def pick(values):
        got = jnp.int32(values[0])
        for i in range(1, ctx_size):
            got = jnp.where(z == i, jnp.int32(values[i]), got)
        return got

    def here(r, p):
        return low[r] <= p < high[r]

    def unit_of(h, r):
        return h if h < moved else moved + (h - moved) * (hub + 1) + r

    def whole_plane(a, b):
        return per_core > moved and ((a < hub and b == hub) or (b < hub and a == hub))

    def at(device, plane=None):
        place = {"head": device // sub_size, "sub": device % sub_size}
        if plane is not None:
            place["ctx"] = plane
        return place

    barrier = pltpu.get_barrier_semaphore()
    for step in range(1, plane_devices):
        other = lax.rem(mine + step, plane_devices)
        pl.semaphore_signal(barrier, device_id=at(other), device_id_type=MESH)
    amounts = []
    for a in range(ctx_size):
        amount = plane_devices - 1
        for b in range(ctx_size):
            if a == b or not (whole_plane(a, b) or abs(a - b) == 1):
                continue
            amount += plane_devices if whole_plane(a, b) else sub_size

            @pl.when(z == a)
            def _():
                if whole_plane(a, b):
                    for device in range(plane_devices):
                        pl.semaphore_signal(
                            barrier, device_id=at(device, b), device_id_type=MESH
                        )
                else:
                    for core in range(sub_size):
                        pl.semaphore_signal(
                            barrier, device_id={"ctx": b, "sub": core}, device_id_type=MESH
                        )

        amounts.append(amount)
    pl.semaphore_wait(barrier, pick(amounts))

    def q_cols(device, h):
        return pl.ds(pl.multiple_of((device * per_core + h) * width, width), width)

    def q_copy(h, step):
        other = lax.rem(mine + step, plane_devices)
        return pltpu.make_async_remote_copy(
            src_ref=q_hbm.at[:, q_cols(other, h)],
            dst_ref=qbuf.at[unit_of(h, hub), mine],
            send_sem=q_send.at[h, step],
            recv_sem=q_recv.at[unit_of(h, hub), mine],
            device_id=at(other),
            device_id_type=MESH,
        )

    def q_own(h):
        return pltpu.make_async_copy(
            q_hbm.at[:, q_cols(mine, h)],
            qbuf.at[unit_of(h, hub), mine],
            q_recv.at[unit_of(h, hub), mine],
        )

    def q_up(h, step):
        other = lax.rem(mine + step, plane_devices)
        unit = unit_of(h, lax.rem(z, hub + 1))
        return pltpu.make_async_remote_copy(
            src_ref=q_hbm.at[:, q_cols(other, h)],
            dst_ref=qbuf.at[unit, mine],
            send_sem=q_send.at[h, step],
            recv_sem=q_recv.at[unit, mine],
            device_id=at(other, hub),
            device_id_type=MESH,
        )

    def o_copy(h, step):
        other = lax.rem(mine + step, plane_devices)
        return pltpu.make_async_remote_copy(
            src_ref=obuf.at[unit_of(h, hub), other],
            dst_ref=out_hbm.at[:, q_cols(mine, h)],
            send_sem=o_send.at[unit_of(h, hub), step],
            recv_sem=o_recv.at[h, mine],
            device_id=at(other),
            device_id_type=MESH,
        )

    def o_own(h):
        return pltpu.make_async_copy(
            obuf.at[unit_of(h, hub), mine], out_hbm.at[:, q_cols(mine, h)], o_recv.at[h, mine]
        )

    def o_down(h, r, step):
        other = lax.rem(mine + step, plane_devices)
        return pltpu.make_async_remote_copy(
            src_ref=obuf.at[unit_of(h, r), other],
            dst_ref=out_hbm.at[:, q_cols(mine, h)],
            send_sem=o_send.at[unit_of(h, r), step],
            recv_sem=o_recv.at[h, mine],
            device_id=at(other, r),
            device_id_type=MESH,
        )

    def kv_source(h, k, p, core):
        row = p % pages_here * PAGE
        col = (core * per_core + h) * HD
        return kv_hbm.at[k, pl.ds(row, PAGE), pl.ds(pl.multiple_of(col, HD), HD)]

    def kv_remote(h, k, p, slot, core, target):
        return pltpu.make_async_remote_copy(
            src_ref=kv_source(h, k, p, core),
            dst_ref=kvbuf.at[h, k, p],
            send_sem=kv_send.at[h, k, slot, p],
            recv_sem=kv_recv.at[h, k, p],
            device_id=target,
            device_id_type=MESH,
        )

    def kv_own(h, k, p):
        return pltpu.make_async_copy(
            kv_source(h, k, p, s), kvbuf.at[h, k, p], kv_recv.at[h, k, p]
        )

    def uses(h, r, p):
        if h < moved:
            return here(r, p)
        return r >= hub and any(here(i, p) for i in (range(hub + 1) if r == hub else [r]))

    def hands_down(h, r, p):
        return any(uses(h, i, p) for i in range(r))

    def each_source(h, k, remote_act, own_act):
        for p in range(live):
            @pl.when((z == plane_of[p]) & (s == core_of[p]))
            def _():
                if hands_down(h, plane_of[p], p):
                    for core in range(sub_size):
                        remote_act(
                            kv_remote(h, k, p, core, core, {"ctx": z - 1, "sub": core})
                        )
                if uses(h, plane_of[p], p):
                    for step in range(1, sub_size):
                        other = lax.rem(s + step, sub_size)
                        remote_act(
                            kv_remote(h, k, p, sub_size - 1 + step, other, {"sub": other})
                        )
                    if own_act is not None:
                        own_act(kv_own(h, k, p))

    def relay(h, k, p):
        return pltpu.make_async_remote_copy(
            src_ref=kvbuf.at[h, k, p],
            dst_ref=kvbuf.at[h, k, p],
            send_sem=relay_send.at[h, k, p],
            recv_sem=kv_recv.at[h, k, p],
            device_id={"ctx": z - 1},
            device_id_type=MESH,
        )

    def bounds(pages):
        return (
            pick([t[0] if t else 0 for t in pages]),
            pick([t[-1] + 1 if t else 0 for t in pages]),
        )

    def take_bounds(h):
        return bounds(
            [
                [
                    p
                    for p in range(live)
                    if uses(h, r, p) or (plane_of[p] > r and hands_down(h, r, p))
                ]
                for r in range(ctx_size)
            ]
        )

    def pass_bounds(h):
        return bounds(
            [
                [p for p in range(live) if plane_of[p] > r and hands_down(h, r, p)]
                for r in range(ctx_size)
            ]
        )

    token = lax.broadcasted_iota(jnp.int32, (QR, PAGE), 0)
    column = lax.broadcasted_iota(jnp.int32, (QR, PAGE), 1)
    factor = HD ** (-0.5) * math.log2(math.e)
    block = ROW_BLOCK
    heads_in_block = block // QR

    def span_of(r):
        first, count = jnp.int32(0), jnp.int32(0)
        for i in range(REQS):
            first = first + jnp.where(r > i, counts_ref[i], 0)
            count = count + jnp.where(r == i, counts_ref[i], 0)
        return first * PAGE, (first + count) * PAGE - QR

    def load_queries(h, unit):
        for device in range(plane_devices):
            pltpu.make_async_copy(
                q_hbm.at[:, q_cols(0, h)], qbuf.at[unit, device], q_recv.at[unit, device]
            ).wait()
        for j in range(group):
            for device in range(plane_devices):
                qs[pl.ds(j * QR + device * tok_rows, tok_rows), :] = qbuf[
                    unit, device, :, j * HD : (j + 1) * HD
                ]
        mx[...] = jnp.full_like(mx, NEG)

    def close_maxima():
        for b in range(rows // block):
            sl = pl.ds(b * block, block)
            mx[sl, :] = jnp.broadcast_to(jnp.max(mx[sl, :], axis=1, keepdims=True), (block, HD))
        lsum[...] = jnp.zeros_like(lsum)
        acc[...] = jnp.zeros_like(acc)

    def score_page(h, p, slot, span):
        first_pos, query_base = span
        keys = kvbuf[h, 0, p]
        pos = p * PAGE + column
        seen = (pos >= first_pos) & (pos <= query_base + token)
        bias = jnp.where(seen, 0.0, NEG)
        for b in range(rows // block):
            sl = pl.ds(b * block, block)
            scores = lax.dot_general(
                qs[sl, :], keys, (((1,), (1,)), ((), ())), preferred_element_type=jnp.float32
            )
            scores = scores.reshape(heads_in_block, QR, PAGE) + bias[None]
            scores = scores.reshape(block, PAGE)
            sbuf[slot, sl, :] = scores
            top = mx[sl, :]
            for c in range(PAGE // HD):
                top = jnp.maximum(top, scores[:, c * HD : (c + 1) * HD])
            mx[sl, :] = top

    def value_page(h, p, slot):
        values = kvbuf[h, 1, p]
        for b in range(rows // block):
            sl = pl.ds(b * block, block)
            top = mx[sl, :]
            parts = [
                jnp.exp2((sbuf[slot, sl, c * HD : (c + 1) * HD] - top) * factor)
                for c in range(PAGE // HD)
            ]
            total = lsum[sl, :]
            for part in parts:
                total = total + part
            lsum[sl, :] = total
            weights = jnp.concatenate([part.astype(jnp.bfloat16) for part in parts], axis=1)
            acc[sl, :] += jnp.dot(weights, values, preferred_element_type=jnp.float32)

    def finish(unit):
        for j in range(group):
            sl = pl.ds(j * QR, QR)
            done = acc[sl, :] / jnp.sum(lsum[sl, :], axis=1, keepdims=True)
            done = done.astype(jnp.bfloat16)
            for device in range(plane_devices):
                obuf[unit, device, :, j * HD : (j + 1) * HD] = done[
                    device * tok_rows : (device + 1) * tok_rows, :
                ]

    def await_page(h, k, p):
        pltpu.make_async_copy(
            kv_source(h, k, 0, 0), kvbuf.at[h, k, p], kv_recv.at[h, k, p]
        ).wait()

    def start(copy):
        copy.start()

    def own_queries(h):
        for step in range(1, plane_devices):
            q_copy(h, step).start()
        q_own(h).start()

    def own_outputs(h):
        for step in range(1, plane_devices):
            o_copy(h, step).start()
        o_own(h).start()

    own_span = span_of(z)
    own_low, own_high = pick(low), pick(high)

    def stream(h, k, then=None):
        take_low, take_high = take_bounds(h)
        pass_low, pass_high = pass_bounds(h)

        def turn_page(p, carry):
            await_page(h, k, p)

            @pl.when((p >= pass_low) & (p < pass_high))
            def _():
                relay(h, k, p).start()

            @pl.when((p >= own_low) & (p < own_high))
            def _():
                if k == 0:
                    score_page(h, p, p - own_low, own_span)
                else:
                    value_page(h, p, p - own_low)

            return carry

        lax.fori_loop(take_low, take_high, turn_page, 0)

    def own_head(h, between=None):
        load_queries(h, unit_of(h, hub))
        stream(h, 0)
        if between is not None:
            between()
        close_maxima()
        stream(h, 1)
        finish(unit_of(h, hub))
        own_outputs(h)

    order = [(h, k) for h in range(moved) for k in range(2)]
    rest = [(h, k) for h in range(moved, per_core) for k in range(2)]
    each_source(*order[0], start, start)
    for h in range(moved, per_core):
        @pl.when(z < hub)
        def _():
            for step in range(plane_devices):
                q_up(h, step).start()

    for h in range(moved):
        own_queries(h)
    for h in range(moved, per_core):
        @pl.when(z >= hub)
        def _():
            own_queries(h)

    for h, k in rest:
        if k == 0:
            each_source(h, k, start, start)

    @pl.when(z > hub)
    def _():
        for h, k in order[1:]:
            each_source(h, k, start, start)

    for h, k in rest:
        if k == 1:
            each_source(h, k, start, start)

    def rest_of_order(turn):
        if turn < len(order):

            @pl.when(z <= hub)
            def _():
                each_source(*order[turn], start, start)

    for h in range(moved):
        own_head(h, lambda h=h: rest_of_order(2 * h + 1))
        rest_of_order(2 * h + 2)

    for h in range(moved, per_core):
        @pl.when(z > hub)
        def _():
            own_head(h)

        @pl.when(z == hub)
        def _():
            known = min(p for p in range(live) if uses(h, hub, p))
            for r in range(hub + 1):
                unit = unit_of(h, r)
                span = span_of(r)
                load_queries(h, unit)
                for k in range(2):

                    def arrive(p, carry, k=k):
                        await_page(h, k, p)
                        return carry

                    def turn_page(p, carry, k=k, r=r, span=span):
                        if k == 0:
                            score_page(h, p, p - low[r], span)
                        else:
                            value_page(h, p, p - low[r])
                        return carry

                    lax.fori_loop(known, high[r], arrive, 0)
                    if k == 1:
                        close_maxima()
                    lax.fori_loop(low[r], high[r], turn_page, 0)
                known = high[r]
                finish(unit)
                if r < hub:
                    for step in range(plane_devices):
                        o_down(h, r, step).start()
                else:
                    own_outputs(h)

    for h in range(per_core):
        for device in range(plane_devices):
            pltpu.make_async_copy(
                obuf.at[0, device], out_hbm.at[:, q_cols(0, h)], o_recv.at[h, device]
            ).wait()

        def drain_own():
            for step in range(1, plane_devices):
                q_copy(h, step).wait_send()
                o_copy(h, step).wait_send()

        if h < moved:
            drain_own()
        else:
            pl.when(z >= hub)(drain_own)

            @pl.when(z < hub)
            def _():
                for step in range(plane_devices):
                    q_up(h, step).wait_send()

            @pl.when(z == hub)
            def _():
                for r in range(hub):
                    for step in range(plane_devices):
                        o_down(h, r, step).wait_send()

        for k in range(2):
            each_source(h, k, lambda copy: copy.wait_send(), None)

            def drain(p, carry, h=h, k=k):
                relay(h, k, p).wait_send()
                return carry

            lax.fori_loop(*pass_bounds(h), drain, 0)


def shipped(queries, kv_cache, page_counts):
    ctx_size, sub_size = lax.axis_size("ctx"), lax.axis_size("sub")
    head_size = lax.axis_size("head")
    local_heads = kv_cache.shape[2] // HD
    pages_here = kv_cache.shape[1] // PAGE
    per_core = local_heads // sub_size
    group = HQ // KVH
    live, low, high, plane_of, _ = page_plan(ctx_size, sub_size, pages_here)
    units = per_core - per_core // 2 + per_core // 2 * (plane_of[0] + 1)
    slots = max(b - a for a, b in zip(low, high))
    plane_devices = head_size * sub_size
    tok_rows = queries.shape[0]
    rows = QR * group
    dma = pltpu.SemaphoreType.DMA
    return pl.pallas_call(
        functools.partial(ship_kernel, (ctx_size, sub_size, head_size, pages_here, local_heads)),
        out_shape=jax.ShapeDtypeStruct(queries.shape, jnp.bfloat16),
        in_specs=[
            pl.BlockSpec(memory_space=pltpu.SMEM),
            pl.BlockSpec(memory_space=pl.ANY),
            pl.BlockSpec(memory_space=pl.ANY),
        ],
        out_specs=pl.BlockSpec(memory_space=pl.ANY),
        scratch_shapes=[
            pltpu.VMEM((per_core, 2, live, PAGE, HD), jnp.bfloat16),
            pltpu.VMEM((units, plane_devices, tok_rows, group * HD), jnp.bfloat16),
            pltpu.VMEM((rows, HD), jnp.bfloat16),
            pltpu.VMEM((slots, rows, PAGE), jnp.float32),
            pltpu.VMEM((rows, HD), jnp.float32),
            pltpu.VMEM((rows, HD), jnp.float32),
            pltpu.VMEM((rows, HD), jnp.float32),
            pltpu.VMEM((units, plane_devices, tok_rows, group * HD), jnp.bfloat16),
            dma((per_core, plane_devices)),
            dma((units, plane_devices)),
            dma((units, plane_devices)),
            dma((per_core, plane_devices)),
            dma((per_core, 2, 2 * sub_size - 1, live)),
            dma((per_core, 2, live)),
            dma((per_core, 2, live)),
        ],
        compiler_params=pltpu.CompilerParams(
            collective_id=0, has_side_effects=True, vmem_limit_bytes=67043328
        ),
    )(page_counts, queries, kv_cache)


def solution(mesh):
    specs = dict(
        mesh=mesh,
        in_specs=(
            P(("grp", "ctx", "head", "sub"), None),
            P(None, ("grp", "ctx", "sub"), "head"),
            P("grp"),
        ),
        out_specs=P(("grp", "ctx", "head", "sub"), None),
        check_vma=False,
    )

    def run(queries, kv_cache, page_counts):
        body = shipped if can_ship(mesh, kv_cache.shape[1]) else per_device
        return jax.shard_map(body, **specs)(queries, kv_cache, page_counts)

    return run
```

profile of v0, /device:TPU:8, one launch (start us, length us, event | category | flops | bytes accessed | tf_op | source)
XLA Modules:
  0.0 40.0 jit_solution(13997836672508858350)
XLA Ops:
  0.0 38.1 %shard_map.37 = bf16[16,16384]{1,0:T(8,128)(2,1)} custom-call(s32[4]{0:T(128)} %counts_ref.1, bf16[16,16384]{1,0:T(8,128)(2,1)} %q_hbm.1, bf16[2,512,512]{2,1,0:T(8,128)(2,1)} %kv_hbm.1), custom_call_target="tpu_custom_call" | custom-call | tf_op jit(solution)/shard_map/pallas_call | solution.py:648
  38.2 1.9 %copy.5 = bf16[16,16384]{1,0:T(8,128)(2,1)} copy(bf16[16,16384]{1,0:T(8,128)(2,1)} %shard_map.37) | data formatting | bytes 1048576
where the time goes:
time: 40.4 us; the launch traced here: 40 us
  Pallas kernels  38.1 us (94%)
  local copies, waits for them, and re-layouts  1.87 us (5%)
    pallas_call x1, Pallas kernels, shipped(): pl.pallas_call(functools.partial(ship_kernel, (ctx_size, sub_size, head_s...  38.1 us
    unnamed x1, local copies, waits for them, and re-layouts  1.87 us

commit v1 on v0

v1 whole, which is shorter than its diff:
```python
import functools
import math

import jax
import jax.numpy as jnp
from jax import lax
from jax.experimental import pallas as pl
from jax.experimental.pallas import tpu as pltpu
from jax.sharding import PartitionSpec as P

HQ = 128
KVH = 8
HD = 128
REQS = 4
QR = 64
PAGE = 256
SPAN = 256


NEG = -1e30
MESH = pl.DeviceIdType.MESH
VMEM_LIMIT = 67043328


def from_behind(array, axis, by):
    count = lax.axis_size(axis)
    pairs = [(i, i + by) for i in range(count) if 0 <= i + by < count]
    return lax.ppermute(array, axis, pairs)


def per_device(queries, kv_cache, page_counts):
    per_group = HQ // KVH
    local_heads = kv_cache.shape[2] // HD
    ctx_size = lax.axis_size("ctx")
    sub_size = lax.axis_size("sub")
    head_count = lax.axis_size("head")
    tok_rows = queries.shape[0]
    score_scale = HD ** (-0.5)
    regrouped = lax.all_to_all(queries, "head", split_axis=1, concat_axis=0, tiled=True)
    all_queries = lax.all_gather(regrouped, ("ctx", "sub"), axis=0, tiled=True)
    all_queries = all_queries.reshape(SPAN, local_heads, per_group, HD)
    page_ends = jnp.cumsum(page_counts)
    ctx_rows = SPAN // ctx_size
    offsets = jnp.arange(QR, dtype=jnp.int32)
    columns = jnp.arange(PAGE, dtype=jnp.int32)
    flat_index = lax.axis_index("ctx") * sub_size + lax.axis_index("sub")
    pages_here = kv_cache.shape[1] // PAGE
    base_pages = pages_here * ctx_size * sub_size // 2
    initial = (
        jnp.full((SPAN, local_heads, per_group), NEG, jnp.float32),
        jnp.zeros((SPAN, local_heads, per_group), jnp.float32),
        jnp.zeros((SPAN, local_heads, per_group, HD), jnp.float32),
    )
    half_rows = kv_cache.shape[1] // 2
    arrived = from_behind(kv_cache[:, half_rows:], "ctx", -(ctx_size // 2))
    is_lower = lax.axis_index("ctx") < ctx_size // 2
    source_flat = flat_index + ctx_size // 2 * sub_size
    working = jnp.where(is_lower, arrived, kv_cache[:, :half_rows])
    first_page = jnp.where(
        is_lower, source_flat * pages_here + pages_here // 2, flat_index * pages_here
    )
    page_total = working.shape[1] // PAGE

    def add_page(page_turn, running):
        page_index = first_page + page_turn
        relative = page_index - base_pages
        counted = jnp.sum((relative >= page_ends).astype(jnp.int32))
        request = jnp.where(relative < 0, REQS, counted)

        def update(partial_value):
            run_max, run_sum, run_out = partial_value
            request_id = jnp.minimum(request, REQS - 1)
            row_start = request_id * QR
            gathered = row_start + offsets
            within = gathered % ctx_rows
            ctx_block = gathered // ctx_rows
            sub_part = within // (head_count * tok_rows)
            head_part = within // tok_rows % head_count
            tok_part = within % tok_rows
            natural = ctx_block * ctx_rows + (head_part * sub_size + sub_part) * tok_rows + tok_part
            query_pos = (page_ends[request_id] + base_pages) * PAGE - QR + natural - row_start
            key_pos = page_index * PAGE + columns
            visible = key_pos[None, :] <= query_pos[:, None]
            page_keys = working[0].reshape(PAGE, local_heads, HD)
            page_values = working[1].reshape(PAGE, local_heads, HD)
            query_rows = lax.dynamic_slice_in_dim(all_queries, row_start, QR, 0)
            scores = (
                jnp.einsum(
                    "qkgd,pkd->qkgp", query_rows, page_keys, preferred_element_type=jnp.float32
                )
                * score_scale
            )
            scores = jnp.where(visible[:, None, None, :], scores, NEG)
            old_max = lax.dynamic_slice_in_dim(run_max, row_start, QR, 0)
            old_sum = lax.dynamic_slice_in_dim(run_sum, row_start, QR, 0)
            old_out = lax.dynamic_slice_in_dim(run_out, row_start, QR, 0)
            new_max = jnp.maximum(old_max, jnp.max(scores, axis=3))
            factor = jnp.exp(old_max - new_max)
            numerators = jnp.exp(scores - new_max[..., None])
            new_sum = old_sum * factor + jnp.sum(numerators, axis=3)
            product = jnp.einsum(
                "qkgp,pkd->qkgd",
                numerators.astype(jnp.bfloat16),
                page_values,
                preferred_element_type=jnp.float32,
            )
            new_out = old_out * factor[..., None] + product
            return (
                lax.dynamic_update_slice_in_dim(run_max, new_max, row_start, 0),
                lax.dynamic_update_slice_in_dim(run_sum, new_sum, row_start, 0),
                lax.dynamic_update_slice_in_dim(run_out, new_out, row_start, 0),
            )

        def unchanged(partial_value):
            return partial_value

        return lax.cond(request < REQS, update, unchanged, running)

    run_max, run_sum, run_out = lax.fori_loop(0, page_total, add_page, initial)
    share = SPAN // (ctx_size * sub_size)
    global_max = lax.pmax(run_max, ("ctx", "sub"))
    factor = jnp.exp(run_max - global_max)
    sums_here, outs_here = (
        lax.psum_scatter(
            (run_sum * factor).astype(jnp.bfloat16), ("ctx", "sub"), scatter_dimension=0, tiled=True
        ).astype(jnp.float32),
        lax.psum_scatter(
            (run_out * factor[..., None]).astype(jnp.bfloat16),
            ("ctx", "sub"),
            scatter_dimension=0,
            tiled=True,
        ).astype(jnp.float32),
    )
    finished = (outs_here / sums_here[..., None]).astype(jnp.bfloat16)
    finished = finished.reshape(share, local_heads * per_group * HD)
    return lax.all_to_all(finished, "head", split_axis=0, concat_axis=1, tiled=True)


FAR, NEAR, HUB, TOP = range(4)


def can_serve(mesh, rows):
    ctx_size, sub_size, head_size = mesh.shape["ctx"], mesh.shape["sub"], mesh.shape["head"]
    if ctx_size != REQS or SPAN // ctx_size != QR or sub_size != 2:
        return False
    pages_here = rows // (mesh.shape["grp"] * ctx_size * sub_size) // PAGE
    return pages_here == 2 and KVH == 2 * head_size * sub_size


def serve_kernel(
    sizes,
    counts_ref,
    q_hbm,
    kv_hbm,
    out_ref,
    kvbuf,
    qbuf,
    obuf,
    sbuf,
    q_send,
    q_recv,
    o_send,
    o_recv,
    kv_send,
    kv_recv,
    go,
):
    head_size, sub_size, pages_here = sizes
    mates = head_size * sub_size
    per_core = KVH // mates
    group = HQ // KVH
    width = group * HD
    tok_rows = QR // mates
    rows = group * tok_rows
    split = pages_here * sub_size
    live = 2 * split
    z, x, s = lax.axis_index("ctx"), lax.axis_index("head"), lax.axis_index("sub")
    mine = x * sub_size + s
    slot_of = jnp.minimum(z, HUB)
    factor = HD ** (-0.5) * math.log2(math.e)

    def at(device, plane=None):
        place = {"head": device // sub_size, "sub": device % sub_size}
        if plane is not None:
            place["ctx"] = plane
        return place

    barrier = pltpu.get_barrier_semaphore()

    def greet(place):
        pl.semaphore_signal(barrier, device_id=place, device_id_type=MESH)

    def greet_plane(plane):
        for device in range(mates):
            greet(at(device, plane))

    def greet_mates():
        for step in range(1, mates):
            greet(at(lax.rem(mine + step, mates)))

    @pl.when(z == HUB)
    def _():
        greet_plane(NEAR)
        greet_plane(FAR)
        greet_mates()
        for core in range(sub_size):
            greet({"ctx": TOP, "sub": core})
        pl.semaphore_wait(barrier, 3 * mates - 1)

    @pl.when(z == TOP)
    def _():
        greet_mates()
        pl.semaphore_wait(barrier, mates - 1 + sub_size)

    @pl.when(z == NEAR)
    def _():
        greet_plane(HUB)
        greet({"ctx": FAR})
        pl.semaphore_wait(barrier, mates)

    @pl.when(z == FAR)
    def _():
        greet_plane(HUB)
        greet_mates()
        pl.semaphore_wait(barrier, 2 * mates)

    def cols(device, h):
        return pl.ds(pl.multiple_of((device * per_core + h) * width, width), width)

    def q_remote(h, step, plane):
        other = lax.rem(mine + step, mates)
        return pltpu.make_async_remote_copy(
            src_ref=q_hbm.at[:, cols(other, h)],
            dst_ref=qbuf.at[slot_of, h, mine],
            send_sem=q_send.at[h, step],
            recv_sem=q_recv.at[slot_of, h, mine],
            device_id=at(other, plane),
            device_id_type=MESH,
        )

    def q_local(h):
        return pltpu.make_async_copy(
            q_hbm.at[:, cols(mine, h)], qbuf.at[slot_of, h, mine], q_recv.at[slot_of, h, mine]
        )

    def q_await(slot, h, device):
        pltpu.make_async_copy(
            q_hbm.at[:, cols(0, 0)], qbuf.at[slot, h, device], q_recv.at[slot, h, device]
        ).wait()

    def o_remote(slot, h, device, plane):
        return pltpu.make_async_remote_copy(
            src_ref=obuf.at[slot, h, device],
            dst_ref=out_ref.at[:, cols(mine, h)],
            send_sem=o_send.at[slot, h, device],
            recv_sem=o_recv.at[h, mine],
            device_id=at(device, plane),
            device_id_type=MESH,
        )

    def o_local(slot, h):
        return pltpu.make_async_copy(
            obuf.at[slot, h, mine], out_ref.at[:, cols(mine, h)], o_recv.at[h, mine]
        )

    def kv_block(k, local, core, h):
        return kv_hbm.at[
            k,
            pl.ds(local * PAGE, PAGE),
            pl.ds(pl.multiple_of((core * per_core + h) * HD, HD), HD),
        ]

    def kv_place(h, k, p):
        return kvbuf.at[h, k, pl.ds(pl.multiple_of(p * PAGE, PAGE), PAGE)]

    def kv_remote(kind, h, k, local, p, core, target):
        return pltpu.make_async_remote_copy(
            src_ref=kv_block(k, local, core, h),
            dst_ref=kv_place(h, k, p),
            send_sem=kv_send.at[kind, h, k, local],
            recv_sem=kv_recv.at[h, k, p],
            device_id=target,
            device_id_type=MESH,
        )

    def kv_local(h, k, local, p):
        return pltpu.make_async_copy(
            kv_block(k, local, s, h), kv_place(h, k, p), kv_recv.at[h, k, p]
        )

    def kv_await(h, pages):
        for k in range(2):
            for p in pages:
                pltpu.make_async_copy(
                    kv_block(0, 0, 0, 0), kv_place(h, k, p), kv_recv.at[h, k, p]
                ).wait()

    def first_local():
        return (s + jnp.where(z == TOP, sub_size, 0)) * pages_here

    def exchange(act, local_act):
        first = first_local()
        for h in range(per_core):
            for k in range(2):
                for local in range(pages_here):
                    act(kv_remote(0, h, k, local, first + local, 1 - s, {"sub": 1 - s}))
                    if local_act is not None:
                        local_act(kv_local(h, k, local, first + local))

    def hand_far(act):
        h = per_core - 1
        for k in range(2):
            for local in range(pages_here):
                act(
                    kv_remote(
                        1, h, k, local, first_local() + local, sub_size - 1,
                        {"ctx": FAR, "sub": sub_size - 1},
                    )
                )

    def hand_hub(act, held):
        for h in range(per_core):
            for core in range(sub_size):
                for k in range(2):
                    for local in range(held):
                        act(
                            kv_remote(
                                1 + core, h, k, local, first_local() + local, core,
                                {"ctx": HUB, "sub": core},
                            )
                        )

    def start(copy):
        copy.start()

    def sent(copy):
        copy.wait_send()

    def span_of(r):
        first, count = jnp.int32(0), jnp.int32(0)
        for i in range(REQS):
            if i < r:
                first = first + counts_ref[i]
            if i == r:
                count = counts_ref[i]
        return first * PAGE, (first + count) * PAGE - QR

    token = lax.broadcasted_iota(jnp.int32, (tok_rows, PAGE), 0)
    column = lax.broadcasted_iota(jnp.int32, (tok_rows, PAGE), 1)

    def attend(slot, h, device, pages, span):
        first_pos, query_base = span
        last_seen = query_base + device * tok_rows + token
        query = jnp.concatenate(
            [qbuf[slot, h, device, :, j * HD : (j + 1) * HD] for j in range(group)], axis=0
        )
        top = jnp.full((rows, HD), NEG, jnp.float32)
        for n, p in enumerate(pages):
            keys = kvbuf[h, 0, p * PAGE : (p + 1) * PAGE, :]
            pos = p * PAGE + column
            bias = jnp.where((pos >= first_pos) & (pos <= last_seen), 0.0, NEG)
            scores = lax.dot_general(
                query, keys, (((1,), (1,)), ((), ())), preferred_element_type=jnp.float32
            )
            scores = scores.reshape(group, tok_rows, PAGE) + bias[None]
            scores = scores.reshape(rows, PAGE)
            sbuf[:, n * PAGE : (n + 1) * PAGE] = scores
            for c in range(PAGE // HD):
                top = jnp.maximum(top, scores[:, c * HD : (c + 1) * HD])
        top = jnp.broadcast_to(jnp.max(top, axis=1, keepdims=True), (rows, HD))
        total = jnp.zeros((rows, HD), jnp.float32)
        summed = jnp.zeros((rows, HD), jnp.float32)
        for n, p in enumerate(pages):
            parts = []
            for c in range(PAGE // HD):
                low = n * PAGE + c * HD
                parts.append(jnp.exp2((sbuf[:, low : low + HD] - top) * factor))
                total = total + parts[-1]
            weights = jnp.concatenate([part.astype(jnp.bfloat16) for part in parts], axis=1)
            values = kvbuf[h, 1, p * PAGE : (p + 1) * PAGE, :]
            summed = summed + jnp.dot(weights, values, preferred_element_type=jnp.float32)
        done = summed / jnp.sum(total, axis=1, keepdims=True)
        done = done.astype(jnp.bfloat16)
        for j in range(group):
            obuf[slot, h, device, :, j * HD : (j + 1) * HD] = done[
                j * tok_rows : (j + 1) * tok_rows, :
            ]

    def turn(slot, h, i, pages, span, plane, own):
        device = lax.rem(mine - i + mates, mates)
        q_await(slot, h, device)
        attend(slot, h, device, pages, span)
        stays = own & (i == 0)

        @pl.when(stays)
        def _():
            o_local(slot, h).start()

        @pl.when(jnp.logical_not(stays))
        def _():
            o_remote(slot, h, device, plane).start()

    far_pages = range(split)
    near_pages = range(1, live - 2)
    hub_pages = range(2, live - 1)
    top_pages = range(split, live)
    last = per_core - 1

    def stays_far(h, step):
        return (h == last) & (lax.rem(s + step, sub_size) == sub_size - 1)

    @pl.when(z == HUB)
    def _():
        hand_far(start)
        exchange(start, start)

    @pl.when((z == TOP) & (s == 0))
    def _():
        hand_hub(start, pages_here)

    @pl.when(z == TOP)
    def _():
        exchange(start, start)

    @pl.when(z >= HUB)
    def _():
        for h in range(per_core):
            q_local(h).start()
            for step in range(1, mates):
                q_remote(h, step, z).start()

    @pl.when(z == FAR)
    def _():
        for h in range(per_core):
            for step in range(mates):
                if h < last:
                    q_remote(h, step, HUB).start()
                else:
                    keep = stays_far(h, step)

                    @pl.when(jnp.logical_not(keep))
                    def _():
                        q_remote(h, step, HUB).start()

                    @pl.when(keep)
                    def _():
                        if step:
                            q_remote(h, step, FAR).start()
                        else:
                            q_local(h).start()

        for h in range(last):
            for step in range(mates):
                q_remote(h, step, HUB).wait_send()
        pl.semaphore_signal(go, device_id={"ctx": NEAR}, device_id_type=MESH)

    @pl.when(z == NEAR)
    def _():
        pl.semaphore_wait(go, 1)
        for h in range(per_core):
            for step in range(mates):
                q_remote(h, step, HUB).start()

    @pl.when((z == HUB) | ((z == FAR) & (s == sub_size - 1)))
    def _():
        span = span_of(FAR)
        h_low = jnp.where(z == FAR, last, 0)
        h_high = jnp.where((z == HUB) & (s == sub_size - 1), last, per_core)

        def step(n, carry):
            h, i = n // mates, n % mates

            @pl.when(i == 0)
            def _():
                kv_await(h, far_pages)

            turn(FAR, h, i, far_pages, span, FAR, z == FAR)
            return carry

        lax.fori_loop(h_low * mates, h_high * mates, step, 0)

    @pl.when(z == HUB)
    def _():
        @pl.when(s == sub_size - 1)
        def _():
            kv_await(last, far_pages)

        near_span, hub_span = span_of(NEAR), span_of(HUB)

        def head_turn(h, carry):
            kv_await(h, [p for p in near_pages if p >= split])

            def near(i, carry):
                turn(NEAR, h, i, near_pages, near_span, NEAR, False)
                return carry

            lax.fori_loop(0, mates, near, 0)
            kv_await(h, [p for p in hub_pages if p >= split and p not in near_pages])

            def own(i, carry):
                turn(HUB, h, i, hub_pages, hub_span, HUB, True)
                return carry

            lax.fori_loop(0, mates, own, 0)
            return carry

        lax.fori_loop(0, per_core, head_turn, 0)

    @pl.when(z == TOP)
    def _():
        span = span_of(TOP)

        def step(n, carry):
            h, i = n // mates, n % mates

            @pl.when(i == 0)
            def _():
                kv_await(h, top_pages)

            turn(HUB, h, i, top_pages, span, TOP, True)
            return carry

        lax.fori_loop(0, per_core * mates, step, 0)

        @pl.when(s == 0)
        def _():
            hand_hub(sent, pages_here)
            pl.semaphore_signal(go, device_id={"sub": 1}, device_id_type=MESH)

        @pl.when(s == 1)
        def _():
            pl.semaphore_wait(go, 1)
            hand_hub(start, 1)
            hand_hub(sent, 1)

    for h in range(per_core):
        for device in range(mates):
            pltpu.make_async_copy(
                obuf.at[0, 0, 0], out_ref.at[:, cols(device, h)], o_recv.at[h, device]
            ).wait()

    @pl.when(z == HUB)
    def _():
        hand_far(sent)

        def drain(n, carry):
            h, device = n // mates, n % mates
            o_remote(NEAR, h, device, NEAR).wait_send()
            return carry

        lax.fori_loop(0, per_core * mates, drain, 0)

    @pl.when((z == HUB) | ((z == FAR) & (s == sub_size - 1)))
    def _():
        h_low = jnp.where(z == FAR, last, 0)
        h_high = jnp.where((z == HUB) & (s == sub_size - 1), last, per_core)

        def drain(n, carry):
            h, i = n // mates, n % mates

            @pl.when((z == HUB) | (i > 0))
            def _():
                o_remote(FAR, h, lax.rem(mine - i + mates, mates), FAR).wait_send()

            return carry

        lax.fori_loop(h_low * mates, h_high * mates, drain, 0)

    @pl.when(z >= HUB)
    def _():
        exchange(sent, None)
        for h in range(per_core):
            for step in range(1, mates):
                q_remote(h, step, z).wait_send()
                o_remote(HUB, h, lax.rem(mine + step, mates), z).wait_send()

    @pl.when(z == NEAR)
    def _():
        for h in range(per_core):
            for step in range(mates):
                q_remote(h, step, HUB).wait_send()

    @pl.when(z == FAR)
    def _():
        for step in range(mates):
            if step:
                q_remote(last, step, HUB).wait_send()
            else:
                @pl.when(jnp.logical_not(stays_far(last, step)))
                def _():
                    q_remote(last, step, HUB).wait_send()


def served(queries, kv_cache, page_counts):
    ctx_size, sub_size = lax.axis_size("ctx"), lax.axis_size("sub")
    head_size = lax.axis_size("head")
    pages_here = kv_cache.shape[1] // PAGE
    mates = head_size * sub_size
    per_core = KVH // mates
    group = HQ // KVH
    live = pages_here * ctx_size * sub_size // 2
    tok_rows = queries.shape[0]
    slots = ctx_size - 1
    dma = pltpu.SemaphoreType.DMA
    chunk = (slots, per_core, mates, tok_rows, group * HD)
    return pl.pallas_call(
        functools.partial(serve_kernel, (head_size, sub_size, pages_here)),
        out_shape=jax.ShapeDtypeStruct(queries.shape, jnp.bfloat16),
        in_specs=[
            pl.BlockSpec(memory_space=pltpu.SMEM),
            pl.BlockSpec(memory_space=pl.ANY),
            pl.BlockSpec(memory_space=pl.ANY),
        ],
        out_specs=pl.BlockSpec(memory_space=pl.ANY),
        scratch_shapes=[
            pltpu.VMEM((per_core, 2, live * PAGE, HD), jnp.bfloat16),
            pltpu.VMEM(chunk, jnp.bfloat16),
            pltpu.VMEM(chunk, jnp.bfloat16),
            pltpu.VMEM((group * tok_rows, (live - 3) * PAGE), jnp.float32),
            dma((per_core, mates)),
            dma((slots, per_core, mates)),
            dma((slots, per_core, mates)),
            dma((per_core, mates)),
            dma((1 + sub_size, per_core, 2, pages_here)),
            dma((per_core, 2, live)),
            pltpu.SemaphoreType.REGULAR,
        ],
        compiler_params=pltpu.CompilerParams(
            collective_id=0, has_side_effects=True, vmem_limit_bytes=VMEM_LIMIT
        ),
    )(page_counts, queries, kv_cache)


def solution(mesh):
    specs = dict(
        mesh=mesh,
        in_specs=(
            P(("grp", "ctx", "head", "sub"), None),
            P(None, ("grp", "ctx", "sub"), "head"),
            P("grp"),
        ),
        out_specs=P(("grp", "ctx", "head", "sub"), None),
        check_vma=False,
    )

    def run(queries, kv_cache, page_counts):
        body = served if can_serve(mesh, kv_cache.shape[1]) else per_device
        return jax.shard_map(body, **specs)(queries, kv_cache, page_counts)

    return run
```

time: 40.4 us -> 37.8 us (0.936)
  the two profiles are of different devices: /device:TPU:8 before, /device:TPU:16 now
where the time goes in v1:
time: 37.8 us; the launch traced here: 37.6 us
  Pallas kernels  35.7 us (94%)
  local copies, waits for them, and re-layouts  1.87 us (5%)
    pallas_call x1, Pallas kernels, served(): pl.pallas_call(functools.partial(serve_kernel, (head_size, sub_size, page...  35.7 us
    unnamed x1, local copies, waits for them, and re-layouts  1.87 us

profile of v1, /device:TPU:16, one launch (start us, length us, event | category | flops | bytes accessed | tf_op | source)
XLA Modules:
  0.0 37.6 jit_solution(7797350272368291476)
XLA Ops:
  0.0 35.7 %shard_map.37 = bf16[16,16384]{1,0:T(8,128)(2,1)} custom-call(s32[4]{0:T(128)} %counts_ref.1, bf16[16,16384]{1,0:T(8,128)(2,1)} %q_hbm.1, bf16[2,512,512]{2,1,0:T(8,128)(2,1)} %kv_hbm.1), custom_call_target="tpu_custom_call" | custom-call | tf_op jit(solution)/shard_map/pallas_call | solution.py:606
  35.8 1.9 %copy.5 = bf16[16,16384]{1,0:T(8,128)(2,1)} copy(bf16[16,16384]{1,0:T(8,128)(2,1)} %shard_map.37) | data formatting | bytes 1048576

commit v2 on v1

--- a/solution.py
+++ b/solution.py
@@ -19,7 +19,9 @@
 
 NEG = -1e30
 MESH = pl.DeviceIdType.MESH
-VMEM_LIMIT = 67043328
+VMEM_LIMIT = 40000000
+EARLY = 1
+AHEAD = 3
 
 
 def from_behind(array, axis, by):
@@ -157,6 +159,7 @@
     qbuf,
     obuf,
     sbuf,
+    tbuf,
     q_send,
     q_recv,
     o_send,
@@ -318,17 +321,16 @@
                     )
                 )
 
-    def hand_hub(act, held):
-        for h in range(per_core):
-            for core in range(sub_size):
-                for k in range(2):
-                    for local in range(held):
-                        act(
-                            kv_remote(
-                                1 + core, h, k, local, first_local() + local, core,
-                                {"ctx": HUB, "sub": core},
-                            )
+    def hand_hub(act, held, h):
+        for core in range(sub_size):
+            for k in range(2):
+                for local in range(held):
+                    act(
+                        kv_remote(
+                            1 + core, h, k, local, first_local() + local, core,
+                            {"ctx": HUB, "sub": core},
                         )
+                    )
 
     def start(copy):
         copy.start()
@@ -348,8 +350,8 @@
     token = lax.broadcasted_iota(jnp.int32, (tok_rows, PAGE), 0)
     column = lax.broadcasted_iota(jnp.int32, (tok_rows, PAGE), 1)
 
-    def attend(slot, h, device, pages, span):
-        first_pos, query_base = span
+    def score(task, room):
+        slot, h, device, pages, (first_pos, query_base) = task
         last_seen = query_base + device * tok_rows + token
         query = jnp.concatenate(
             [qbuf[slot, h, device, :, j * HD : (j + 1) * HD] for j in range(group)], axis=0
@@ -364,9 +366,13 @@
             )
             scores = scores.reshape(group, tok_rows, PAGE) + bias[None]
             scores = scores.reshape(rows, PAGE)
-            sbuf[:, n * PAGE : (n + 1) * PAGE] = scores
+            room[:, n * PAGE : (n + 1) * PAGE] = scores
             for c in range(PAGE // HD):
                 top = jnp.maximum(top, scores[:, c * HD : (c + 1) * HD])
+        return top
+
+    def weigh(task, room, top):
+        slot, h, device, pages, _ = task
         top = jnp.broadcast_to(jnp.max(top, axis=1, keepdims=True), (rows, HD))
         total = jnp.zeros((rows, HD), jnp.float32)
         summed = jnp.zeros((rows, HD), jnp.float32)
@@ -374,7 +380,7 @@
             parts = []
             for c in range(PAGE // HD):
                 low = n * PAGE + c * HD
-                parts.append(jnp.exp2((sbuf[:, low : low + HD] - top) * factor))
+                parts.append(jnp.exp2((room[:, low : low + HD] - top) * factor))
                 total = total + parts[-1]
             weights = jnp.concatenate([part.astype(jnp.bfloat16) for part in parts], axis=1)
             values = kvbuf[h, 1, p * PAGE : (p + 1) * PAGE, :]
@@ -386,24 +392,32 @@
                 j * tok_rows : (j + 1) * tok_rows, :
             ]
 
+    def attend(*tasks):
+        rooms = (sbuf, tbuf)[: len(tasks)]
+        tops = [score(task, room) for task, room in zip(tasks, rooms)]
+        for task, room, top in zip(tasks, rooms, tops):
+            weigh(task, room, top)
+
+    def send_home(slot, h, device, plane, stays):
+        @pl.when(stays)
+        def _():
+            o_local(slot, h).start()
+
+        @pl.when(jnp.logical_not(stays))
+        def _():
+            o_remote(slot, h, device, plane).start()
+
     def turn(slot, h, i, pages, span, plane, own):
         device = lax.rem(mine - i + mates, mates)
         q_await(slot, h, device)
-        attend(slot, h, device, pages, span)
-        stays = own & (i == 0)
-
-        @pl.when(stays)
-        def _():
-            o_local(slot, h).start()
-
-        @pl.when(jnp.logical_not(stays))
-        def _():
-            o_remote(slot, h, device, plane).start()
+        attend((slot, h, device, pages, span))
+        send_home(slot, h, device, plane, own & (i == 0))
 
     far_pages = range(split)
     near_pages = range(1, live - 2)
     hub_pages = range(2, live - 1)
     top_pages = range(split, live)
+    near_or_hub = {*near_pages, *hub_pages}
     last = per_core - 1
 
     def stays_far(h, step):
@@ -416,7 +430,8 @@
 
     @pl.when((z == TOP) & (s == 0))
     def _():
-        hand_hub(start, pages_here)
+        for h in range(per_core):
+            hand_hub(start, pages_here, h)
 
     @pl.when(z == TOP)
     def _():
@@ -449,17 +464,19 @@
                         else:
                             q_local(h).start()
 
-        for h in range(last):
+        for step in range(AHEAD):
+            q_remote(0, step, HUB).wait_send()
+        pl.semaphore_signal(go, device_id={"ctx": NEAR}, device_id_type=MESH)
+
+    @pl.when(z == NEAR)
+    def _():
+        for step in range(EARLY):
+            q_remote(0, step, HUB).start()
+        pl.semaphore_wait(go, 1)
+        for h in range(per_core):
             for step in range(mates):
-                q_remote(h, step, HUB).wait_send()
-        pl.semaphore_signal(go, device_id={"ctx": NEAR}, device_id_type=MESH)
-
-    @pl.when(z == NEAR)
-    def _():
-        pl.semaphore_wait(go, 1)
-        for h in range(per_core):
-            for step in range(mates):
-                q_remote(h, step, HUB).start()
+                if h or step >= EARLY:
+                    q_remote(h, step, HUB).start()
 
     @pl.when((z == HUB) | ((z == FAR) & (s == sub_size - 1)))
     def _():
@@ -487,24 +504,24 @@
 
         near_span, hub_span = span_of(NEAR), span_of(HUB)
 
-        def head_turn(h, carry):
-            kv_await(h, [p for p in near_pages if p >= split])
-
-            def near(i, carry):
-                turn(NEAR, h, i, near_pages, near_span, NEAR, False)
-                return carry
-
-            lax.fori_loop(0, mates, near, 0)
-            kv_await(h, [p for p in hub_pages if p >= split and p not in near_pages])
-
-            def own(i, carry):
-                turn(HUB, h, i, hub_pages, hub_span, HUB, True)
-                return carry
-
-            lax.fori_loop(0, mates, own, 0)
+        def both(n, carry):
+            h, i = n // mates, n % mates
+
+            @pl.when(i == 0)
+            def _():
+                kv_await(h, [p for p in range(live) if p >= split and p in near_or_hub])
+
+            device = lax.rem(mine - i + mates, mates)
+            q_await(NEAR, h, device)
+            q_await(HUB, h, device)
+            attend(
+                (NEAR, h, device, near_pages, near_span), (HUB, h, device, hub_pages, hub_span)
+            )
+            o_remote(NEAR, h, device, NEAR).start()
+            send_home(HUB, h, device, HUB, i == 0)
             return carry
 
-        lax.fori_loop(0, per_core, head_turn, 0)
+        lax.fori_loop(0, per_core * mates, both, 0)
 
     @pl.when(z == TOP)
     def _():
@@ -518,26 +535,35 @@
                 kv_await(h, top_pages)
 
             turn(HUB, h, i, top_pages, span, TOP, True)
+
+            @pl.when((s == 1) & (i == mates - 1))
+            def _():
+                hand_hub(start, 1, h)
+
             return carry
 
         lax.fori_loop(0, per_core * mates, step, 0)
 
+    def finals():
+        for h in range(per_core):
+            for device in range(mates):
+                pltpu.make_async_copy(
+                    obuf.at[0, 0, 0], out_ref.at[:, cols(device, h)], o_recv.at[h, device]
+                ).wait()
+
+    finals()
+
+    @pl.when(z == TOP)
+    def _():
         @pl.when(s == 0)
         def _():
-            hand_hub(sent, pages_here)
-            pl.semaphore_signal(go, device_id={"sub": 1}, device_id_type=MESH)
+            for h in range(per_core):
+                hand_hub(sent, pages_here, h)
 
         @pl.when(s == 1)
         def _():
-            pl.semaphore_wait(go, 1)
-            hand_hub(start, 1)
-            hand_hub(sent, 1)
-
-    for h in range(per_core):
-        for device in range(mates):
-            pltpu.make_async_copy(
-                obuf.at[0, 0, 0], out_ref.at[:, cols(device, h)], o_recv.at[h, device]
-            ).wait()
+            for h in range(per_core):
+                hand_hub(sent, 1, h)
 
     @pl.when(z == HUB)
     def _():
@@ -582,6 +608,10 @@
 
     @pl.when(z == FAR)
     def _():
+        for h in range(last):
+            for step in range(mates):
+                if h or step >= AHEAD:
+                    q_remote(h, step, HUB).wait_send()
         for step in range(mates):
             if step:
                 q_remote(last, step, HUB).wait_send()
@@ -617,6 +647,7 @@
             pltpu.VMEM(chunk, jnp.bfloat16),
             pltpu.VMEM(chunk, jnp.bfloat16),
             pltpu.VMEM((group * tok_rows, (live - 3) * PAGE), jnp.float32),
+            pltpu.VMEM((group * tok_rows, (live - 3) * PAGE), jnp.float32),
             dma((per_core, mates)),
             dma((slots, per_core, mates)),
             dma((slots, per_core, mates)),
@@ -628,7 +659,11 @@
         compiler_params=pltpu.CompilerParams(
             collective_id=0, has_side_effects=True, vmem_limit_bytes=VMEM_LIMIT
         ),
-    )(page_counts, queries, kv_cache)
+    )(
+        pltpu.with_memory_space_constraint(page_counts, pltpu.HBM),
+        pltpu.with_memory_space_constraint(queries, pltpu.HBM),
+        pltpu.with_memory_space_constraint(kv_cache, pltpu.HBM),
+    )
 
 
 def solution(mesh):

time: 37.8 us -> 34.1 us (0.902)
  the two profiles are of different devices: /device:TPU:16 before, /device:TPU:8 now
where the time goes in v2:
time: 34.1 us; the launch traced here: 34 us
  Pallas kernels  33.2 us (97%)
  local copies, waits for them, and re-layouts  0.8 us (2%)
    pallas_call x1, Pallas kernels, served(): pl.pallas_call(functools.partial(serve_kernel, (head_size, sub_size, page...  33.2 us
    unnamed x1, local copies, waits for them, and re-layouts  0.8 us

profile of v2, /device:TPU:8, one launch (start us, length us, event | category | flops | bytes accessed | tf_op | source)
XLA Modules:
  0.0 34.0 jit_solution(18159993332921259032)
XLA Ops:
  0.0 33.2 %shard_map.37 = bf16[16,16384]{1,0:T(8,128)(2,1)S(1)} custom-call(s32[4]{0:T(128)} %counts_ref.1, bf16[16,16384]{1,0:T(8,128)(2,1)} %q_hbm.1, bf16[2,512,512]{2,1,0:T(8,128)(2,1)} %kv_hbm.1), custom_call_target="tpu_custom_call" | custom-call | tf_op jit(solution)/shard_map/pallas_call | solution.py:636
  33.2 0.8 %copy.5 = bf16[16,16384]{1,0:T(8,128)(2,1)} copy(bf16[16,16384]{1,0:T(8,128)(2,1)S(1)} %shard_map.37) | data formatting | bytes 1048576

commit v3 on v2

--- a/solution.py
+++ b/solution.py
@@ -21,6 +21,7 @@
 MESH = pl.DeviceIdType.MESH
 VMEM_LIMIT = 40000000
 EARLY = 1
+LATER = 4
 AHEAD = 3
 
 
@@ -146,22 +147,25 @@
     if ctx_size != REQS or SPAN // ctx_size != QR or sub_size != 2:
         return False
     pages_here = rows // (mesh.shape["grp"] * ctx_size * sub_size) // PAGE
-    return pages_here == 2 and KVH == 2 * head_size * sub_size
+    return pages_here == 2 and head_size == 2 and KVH == 2 * head_size * sub_size
 
 
 def serve_kernel(
     sizes,
-    counts_ref,
+    counts_hbm,
     q_hbm,
     kv_hbm,
     out_ref,
+    counts_ref,
     kvbuf,
     qbuf,
     obuf,
     sbuf,
     tbuf,
+    counts_sem,
     q_send,
     q_recv,
+    own_recv,
     o_send,
     o_recv,
     kv_send,
@@ -189,6 +193,8 @@
         return place
 
     barrier = pltpu.get_barrier_semaphore()
+    counts_copy = pltpu.make_async_copy(counts_hbm, counts_ref, counts_sem.at[0])
+    counts_copy.start()
 
     def greet(place):
         pl.semaphore_signal(barrier, device_id=place, device_id_type=MESH)
@@ -203,9 +209,9 @@
 
     @pl.when(z == HUB)
     def _():
+        greet_mates()
+        greet_plane(FAR)
         greet_plane(NEAR)
-        greet_plane(FAR)
-        greet_mates()
         for core in range(sub_size):
             greet({"ctx": TOP, "sub": core})
         pl.semaphore_wait(barrier, 3 * mates - 1)
@@ -227,116 +233,105 @@
         greet_mates()
         pl.semaphore_wait(barrier, 2 * mates)
 
+    counts_copy.wait()
+
+    def partner(h, step):
+        turned = jnp.where(h == 0, step, mates - 1 - step)
+        far_x, far_s = turned // sub_size, turned % sub_size
+        return lax.rem(x + far_x, head_size) * sub_size + lax.rem(s + far_s, sub_size)
+
+    def alone(h, step):
+        return jnp.where(h == 0, step, mates - 1 - step) == 0
+
     def cols(device, h):
         return pl.ds(pl.multiple_of((device * per_core + h) * width, width), width)
 
-    def q_remote(h, step, plane):
-        other = lax.rem(mine + step, mates)
+    def q_remote(h, step, plane, recv, part=1):
+        other = partner(h, step)
         return pltpu.make_async_remote_copy(
             src_ref=q_hbm.at[:, cols(other, h)],
             dst_ref=qbuf.at[slot_of, h, mine],
-            send_sem=q_send.at[h, step],
-            recv_sem=q_recv.at[slot_of, h, mine],
+            send_sem=q_send.at[part],
+            recv_sem=recv,
             device_id=at(other, plane),
             device_id_type=MESH,
         )
 
-    def q_local(h):
-        return pltpu.make_async_copy(
-            q_hbm.at[:, cols(mine, h)], qbuf.at[slot_of, h, mine], q_recv.at[slot_of, h, mine]
-        )
+    def q_local(h, recv):
+        return pltpu.make_async_copy(q_hbm.at[:, cols(mine, h)], qbuf.at[slot_of, h, mine], recv)
 
     def q_await(slot, h, device):
         pltpu.make_async_copy(
             q_hbm.at[:, cols(0, 0)], qbuf.at[slot, h, device], q_recv.at[slot, h, device]
         ).wait()
 
+    def own_await(h):
+        pltpu.make_async_copy(obuf.at[HUB, h], qbuf.at[HUB, h], own_recv.at[h]).wait()
+
     def o_remote(slot, h, device, plane):
         return pltpu.make_async_remote_copy(
             src_ref=obuf.at[slot, h, device],
             dst_ref=out_ref.at[:, cols(mine, h)],
-            send_sem=o_send.at[slot, h, device],
-            recv_sem=o_recv.at[h, mine],
+            send_sem=o_send.at[slot],
+            recv_sem=o_recv.at[0],
             device_id=at(device, plane),
             device_id_type=MESH,
         )
 
     def o_local(slot, h):
         return pltpu.make_async_copy(
-            obuf.at[slot, h, mine], out_ref.at[:, cols(mine, h)], o_recv.at[h, mine]
+            obuf.at[slot, h, mine], out_ref.at[:, cols(mine, h)], o_recv.at[0]
         )
 
-    def kv_block(k, local, core, h):
+    def settle(sem, chunks):
+        span = pl.ds(0, chunks * width)
+        pltpu.make_async_copy(q_hbm.at[:, span], out_ref.at[:, span], sem).wait()
+
+    def settle_kv(blocks):
+        span = pl.ds(0, blocks * PAGE // (2 * per_core))
+        pltpu.make_async_copy(kvbuf.at[:, :, span], kvbuf.at[:, :, span], kv_send.at[0]).wait()
+
+    def kv_block(core, h, held):
         return kv_hbm.at[
-            k,
-            pl.ds(local * PAGE, PAGE),
+            :,
+            pl.ds(0, held * PAGE),
             pl.ds(pl.multiple_of((core * per_core + h) * HD, HD), HD),
         ]
 
-    def kv_place(h, k, p):
-        return kvbuf.at[h, k, pl.ds(pl.multiple_of(p * PAGE, PAGE), PAGE)]
-
-    def kv_remote(kind, h, k, local, p, core, target):
+    def kv_place(h, p, held):
+        return kvbuf.at[h, :, pl.ds(pl.multiple_of(p * PAGE, PAGE), held * PAGE)]
+
+    here = (s + jnp.where(z == TOP, sub_size, 0)) * pages_here
+    half = jnp.where(z == TOP, 1, 0)
+
+    def kv_remote(h, core, held, target):
         return pltpu.make_async_remote_copy(
-            src_ref=kv_block(k, local, core, h),
-            dst_ref=kv_place(h, k, p),
-            send_sem=kv_send.at[kind, h, k, local],
-            recv_sem=kv_recv.at[h, k, p],
+            src_ref=kv_block(core, h, held),
+            dst_ref=kv_place(h, here, held),
+            send_sem=kv_send.at[0],
+            recv_sem=kv_recv.at[h, half],
             device_id=target,
             device_id_type=MESH,
         )
 
-    def kv_local(h, k, local, p):
-        return pltpu.make_async_copy(
-            kv_block(k, local, s, h), kv_place(h, k, p), kv_recv.at[h, k, p]
-        )
-
-    def kv_await(h, pages):
-        for k in range(2):
-            for p in pages:
-                pltpu.make_async_copy(
-                    kv_block(0, 0, 0, 0), kv_place(h, k, p), kv_recv.at[h, k, p]
-                ).wait()
-
-    def first_local():
-        return (s + jnp.where(z == TOP, sub_size, 0)) * pages_here
-
-    def exchange(act, local_act):
-        first = first_local()
+    def kv_await(h, first, count):
+        place = kv_place(h, first, count)
+        pltpu.make_async_copy(place, place, kv_recv.at[h, 0 if first < split else 1]).wait()
+
+    def exchange():
         for h in range(per_core):
-            for k in range(2):
-                for local in range(pages_here):
-                    act(kv_remote(0, h, k, local, first + local, 1 - s, {"sub": 1 - s}))
-                    if local_act is not None:
-                        local_act(kv_local(h, k, local, first + local))
-
-    def hand_far(act):
-        h = per_core - 1
-        for k in range(2):
-            for local in range(pages_here):
-                act(
-                    kv_remote(
-                        1, h, k, local, first_local() + local, sub_size - 1,
-                        {"ctx": FAR, "sub": sub_size - 1},
-                    )
-                )
-
-    def hand_hub(act, held, h):
-        for core in range(sub_size):
-            for k in range(2):
-                for local in range(held):
-                    act(
-                        kv_remote(
-                            1 + core, h, k, local, first_local() + local, core,
-                            {"ctx": HUB, "sub": core},
-                        )
-                    )
-
-    def start(copy):
-        copy.start()
-
-    def sent(copy):
-        copy.wait_send()
+            kv_remote(h, 1 - s, pages_here, {"sub": 1 - s}).start()
+            pltpu.make_async_copy(
+                kv_block(s, h, pages_here), kv_place(h, here, pages_here), kv_recv.at[h, half]
+            ).start()
+
+    def hand_far():
+        core = sub_size - 1
+        kv_remote(per_core - 1, core, pages_here, {"ctx": FAR, "sub": core}).start()
+
+    def hand_hub(held, h):
+        for core in reversed(range(sub_size)):
+            kv_remote(h, core, held, {"ctx": HUB, "sub": core}).start()
 
     def span_of(r):
         first, count = jnp.int32(0), jnp.int32(0)
@@ -408,75 +403,78 @@
             o_remote(slot, h, device, plane).start()
 
     def turn(slot, h, i, pages, span, plane, own):
-        device = lax.rem(mine - i + mates, mates)
-        q_await(slot, h, device)
+        device = partner(h, i)
         attend((slot, h, device, pages, span))
-        send_home(slot, h, device, plane, own & (i == 0))
+        send_home(slot, h, device, plane, own & alone(h, i))
 
     far_pages = range(split)
     near_pages = range(1, live - 2)
     hub_pages = range(2, live - 1)
     top_pages = range(split, live)
-    near_or_hub = {*near_pages, *hub_pages}
     last = per_core - 1
 
-    def stays_far(h, step):
-        return (h == last) & (lax.rem(s + step, sub_size) == sub_size - 1)
+    def stays_far(step):
+        return lax.rem(partner(last, step), sub_size) == sub_size - 1
 
     @pl.when(z == HUB)
     def _():
-        hand_far(start)
-        exchange(start, start)
+        hand_far()
+        exchange()
 
     @pl.when((z == TOP) & (s == 0))
     def _():
         for h in range(per_core):
-            hand_hub(start, pages_here, h)
+            hand_hub(pages_here, h)
+
+    @pl.when((z == TOP) & (s == 1))
+    def _():
+        hand_hub(1, 0)
 
     @pl.when(z == TOP)
     def _():
-        exchange(start, start)
+        exchange()
 
     @pl.when(z >= HUB)
     def _():
         for h in range(per_core):
-            q_local(h).start()
-            for step in range(1, mates):
-                q_remote(h, step, z).start()
+            q_local(h, own_recv.at[h]).start()
+            for step in range(mates):
+                if (step, mates - 1 - step)[h != 0]:
+                    q_remote(h, step, z, own_recv.at[h]).start()
 
     @pl.when(z == FAR)
     def _():
         for h in range(per_core):
+            recv = q_recv.at[FAR, h, mine]
             for step in range(mates):
                 if h < last:
-                    q_remote(h, step, HUB).start()
+                    q_remote(h, step, HUB, recv, 0 if step < AHEAD else 1).start()
                 else:
-                    keep = stays_far(h, step)
+                    keep = stays_far(step)
 
                     @pl.when(jnp.logical_not(keep))
                     def _():
-                        q_remote(h, step, HUB).start()
+                        q_remote(h, step, HUB, recv).start()
 
                     @pl.when(keep)
                     def _():
-                        if step:
-                            q_remote(h, step, FAR).start()
+                        if mates - 1 - step:
+                            q_remote(h, step, FAR, recv).start()
                         else:
-                            q_local(h).start()
-
-        for step in range(AHEAD):
-            q_remote(0, step, HUB).wait_send()
+                            q_local(h, recv).start()
+
+        settle(q_send.at[0], AHEAD)
         pl.semaphore_signal(go, device_id={"ctx": NEAR}, device_id_type=MESH)
 
     @pl.when(z == NEAR)
     def _():
         for step in range(EARLY):
-            q_remote(0, step, HUB).start()
+            q_remote(0, step, HUB, q_recv.at[NEAR, 0, mine]).start()
         pl.semaphore_wait(go, 1)
         for h in range(per_core):
             for step in range(mates):
                 if h or step >= EARLY:
-                    q_remote(h, step, HUB).start()
+                    q_remote(h, step, HUB, q_recv.at[NEAR, h, mine]).start()
 
     @pl.when((z == HUB) | ((z == FAR) & (s == sub_size - 1)))
     def _():
@@ -489,8 +487,9 @@
 
             @pl.when(i == 0)
             def _():
-                kv_await(h, far_pages)
-
+                kv_await(h, 0, split)
+
+            q_await(FAR, h, partner(h, i))
             turn(FAR, h, i, far_pages, span, FAR, z == FAR)
             return carry
 
@@ -500,7 +499,7 @@
     def _():
         @pl.when(s == sub_size - 1)
         def _():
-            kv_await(last, far_pages)
+            kv_await(last, 0, split)
 
         near_span, hub_span = span_of(NEAR), span_of(HUB)
 
@@ -509,16 +508,16 @@
 
             @pl.when(i == 0)
             def _():
-                kv_await(h, [p for p in range(live) if p >= split and p in near_or_hub])
-
-            device = lax.rem(mine - i + mates, mates)
+                own_await(h)
+                kv_await(h, split, split - 1)
+
+            device = partner(h, i)
             q_await(NEAR, h, device)
-            q_await(HUB, h, device)
             attend(
                 (NEAR, h, device, near_pages, near_span), (HUB, h, device, hub_pages, hub_span)
             )
             o_remote(NEAR, h, device, NEAR).start()
-            send_home(HUB, h, device, HUB, i == 0)
+            send_home(HUB, h, device, HUB, alone(h, i))
             return carry
 
         lax.fori_loop(0, per_core * mates, both, 0)
@@ -532,93 +531,64 @@
 
             @pl.when(i == 0)
             def _():
-                kv_await(h, top_pages)
+                own_await(h)
+                kv_await(h, split, split)
 
             turn(HUB, h, i, top_pages, span, TOP, True)
 
-            @pl.when((s == 1) & (i == mates - 1))
+            @pl.when((s == 1) & (n == LATER))
             def _():
-                hand_hub(start, 1, h)
+                hand_hub(1, last)
 
             return carry
 
         lax.fori_loop(0, per_core * mates, step, 0)
 
     def finals():
-        for h in range(per_core):
-            for device in range(mates):
-                pltpu.make_async_copy(
-                    obuf.at[0, 0, 0], out_ref.at[:, cols(device, h)], o_recv.at[h, device]
-                ).wait()
+        settle(o_recv.at[0], per_core * mates)
 
     finals()
 
-    @pl.when(z == TOP)
-    def _():
+    @pl.when(z == HUB)
+    def _():
+        settle_kv(2 * pages_here * (per_core + 1))
+        settle(o_send.at[NEAR], per_core * mates)
+
         @pl.when(s == 0)
         def _():
-            for h in range(per_core):
-                hand_hub(sent, pages_here, h)
+            settle(o_send.at[FAR], per_core * mates)
 
         @pl.when(s == 1)
         def _():
-            for h in range(per_core):
-                hand_hub(sent, 1, h)
-
-    @pl.when(z == HUB)
-    def _():
-        hand_far(sent)
-
-        def drain(n, carry):
-            h, device = n // mates, n % mates
-            o_remote(NEAR, h, device, NEAR).wait_send()
-            return carry
-
-        lax.fori_loop(0, per_core * mates, drain, 0)
-
-    @pl.when((z == HUB) | ((z == FAR) & (s == sub_size - 1)))
-    def _():
-        h_low = jnp.where(z == FAR, last, 0)
-        h_high = jnp.where((z == HUB) & (s == sub_size - 1), last, per_core)
-
-        def drain(n, carry):
-            h, i = n // mates, n % mates
-
-            @pl.when((z == HUB) | (i > 0))
-            def _():
-                o_remote(FAR, h, lax.rem(mine - i + mates, mates), FAR).wait_send()
-
-            return carry
-
-        lax.fori_loop(h_low * mates, h_high * mates, drain, 0)
+            settle(o_send.at[FAR], last * mates)
+
+    @pl.when(z == TOP)
+    def _():
+        @pl.when(s == 0)
+        def _():
+            settle_kv(2 * pages_here * per_core * (1 + sub_size))
+
+        @pl.when(s == 1)
+        def _():
+            settle_kv(2 * per_core * (pages_here + sub_size))
 
     @pl.when(z >= HUB)
     def _():
-        exchange(sent, None)
-        for h in range(per_core):
-            for step in range(1, mates):
-                q_remote(h, step, z).wait_send()
-                o_remote(HUB, h, lax.rem(mine + step, mates), z).wait_send()
+        settle(q_send.at[1], per_core * (mates - 1))
+        settle(o_send.at[HUB], per_core * (mates - 1))
 
     @pl.when(z == NEAR)
     def _():
-        for h in range(per_core):
-            for step in range(mates):
-                q_remote(h, step, HUB).wait_send()
-
-    @pl.when(z == FAR)
-    def _():
-        for h in range(last):
-            for step in range(mates):
-                if h or step >= AHEAD:
-                    q_remote(h, step, HUB).wait_send()
-        for step in range(mates):
-            if step:
-                q_remote(last, step, HUB).wait_send()
-            else:
-                @pl.when(jnp.logical_not(stays_far(last, step)))
-                def _():
-                    q_remote(last, step, HUB).wait_send()
+        settle(q_send.at[1], per_core * mates)
+
+    @pl.when((z == FAR) & (s == 0))
+    def _():
+        settle(q_send.at[1], per_core * mates - AHEAD)
+
+    @pl.when((z == FAR) & (s == 1))
+    def _():
+        settle(q_send.at[1], per_core * mates - 1 - AHEAD)
+        settle(o_send.at[FAR], mates - 1)
 
 
 def served(queries, kv_cache, page_counts):
@@ -637,23 +607,26 @@
         functools.partial(serve_kernel, (head_size, sub_size, pages_here)),
         out_shape=jax.ShapeDtypeStruct(queries.shape, jnp.bfloat16),
         in_specs=[
-            pl.BlockSpec(memory_space=pltpu.SMEM),
+            pl.BlockSpec(memory_space=pl.ANY),
             pl.BlockSpec(memory_space=pl.ANY),
             pl.BlockSpec(memory_space=pl.ANY),
         ],
         out_specs=pl.BlockSpec(memory_space=pl.ANY),
         scratch_shapes=[
+            pltpu.SMEM((REQS,), jnp.int32),
             pltpu.VMEM((per_core, 2, live * PAGE, HD), jnp.bfloat16),
             pltpu.VMEM(chunk, jnp.bfloat16),
             pltpu.VMEM(chunk, jnp.bfloat16),
             pltpu.VMEM((group * tok_rows, (live - 3) * PAGE), jnp.float32),
             pltpu.VMEM((group * tok_rows, (live - 3) * PAGE), jnp.float32),
-            dma((per_core, mates)),
-            dma((slots, per_core, mates)),
-            dma((slots, per_core, mates)),
-            dma((per_core, mates)),
-            dma((1 + sub_size, per_core, 2, pages_here)),
-            dma((per_core, 2, live)),
+            dma((1,)),
+            dma((2,)),
+            dma((slots - 1, per_core, mates)),
+            dma((per_core,)),
+            dma((slots,)),
+            dma((1,)),
+            dma((1,)),
+            dma((per_core, 2)),
             pltpu.SemaphoreType.REGULAR,
         ],
         compiler_params=pltpu.CompilerParams(

time: 34.1 us -> 31.3 us (0.918)
  Pallas kernels: 33.2 us -> 30.4 us
    pallas_call x1, Pallas kernels: 33.2 us -> 30.4 us  [served(): pl.pallas_call(functools.partial(serve_kernel, (head_size, sub_size, page...]
where the time goes in v3:
time: 31.3 us; the launch traced here: 31.2 us
  Pallas kernels  30.4 us (97%)
  local copies, waits for them, and re-layouts  0.8 us (3%)
    pallas_call x1, Pallas kernels, served(): pl.pallas_call(functools.partial(serve_kernel, (head_size, sub_size, page...  30.4 us
    unnamed x1, local copies, waits for them, and re-layouts  0.8 us

profile of v3, /device:TPU:8, one launch (start us, length us, event | category | flops | bytes accessed | tf_op | source)
XLA Modules:
  0.0 31.2 jit_solution(9293467453124835979)
XLA Ops:
  0.0 30.4 %shard_map.37 = bf16[16,16384]{1,0:T(8,128)(2,1)S(1)} custom-call(s32[4]{0:T(128)} %counts_hbm.1, bf16[16,16384]{1,0:T(8,128)(2,1)} %q_hbm.1, bf16[2,512,512]{2,1,0:T(8,128)(2,1)} %kv_hbm.1), custom_call_target="tpu_custom_call" | custom-call | tf_op jit(solution)/shard_map/pallas_call | solution.py:606
  30.4 0.8 %copy.5 = bf16[16,16384]{1,0:T(8,128)(2,1)} copy(bf16[16,16384]{1,0:T(8,128)(2,1)S(1)} %shard_map.37) | data formatting | bytes 1048576

commit v4 on v3

--- a/solution.py
+++ b/solution.py
@@ -21,7 +21,9 @@
 MESH = pl.DeviceIdType.MESH
 VMEM_LIMIT = 40000000
 EARLY = 1
-LATER = 4
+WHEN = 2
+OWN = 2
+LAG = 2
 AHEAD = 3
 
 
@@ -203,37 +205,42 @@
         for device in range(mates):
             greet(at(device, plane))
 
+    def greet_column(plane):
+        for core in range(sub_size):
+            greet({"ctx": plane, "sub": core})
+
     def greet_mates():
         for step in range(1, mates):
             greet(at(lax.rem(mine + step, mates)))
 
+    def vouch(plane):
+        pl.semaphore_signal(go, device_id={"ctx": plane}, device_id_type=MESH)
+
     @pl.when(z == HUB)
     def _():
+        greet_column(NEAR)
+        greet_column(FAR)
+        greet_plane(TOP)
+        pl.semaphore_wait(barrier, sub_size)
+
+    @pl.when(z == TOP)
+    def _():
         greet_mates()
-        greet_plane(FAR)
-        greet_plane(NEAR)
-        for core in range(sub_size):
-            greet({"ctx": TOP, "sub": core})
-        pl.semaphore_wait(barrier, 3 * mates - 1)
-
-    @pl.when(z == TOP)
-    def _():
-        greet_mates()
-        pl.semaphore_wait(barrier, mates - 1 + sub_size)
+        pl.semaphore_wait(barrier, 4 * mates - 1)
+        vouch(HUB)
+        vouch(FAR)
+        vouch(NEAR)
 
     @pl.when(z == NEAR)
     def _():
-        greet_plane(HUB)
-        greet({"ctx": FAR})
-        pl.semaphore_wait(barrier, mates)
+        greet_plane(TOP)
+        pl.semaphore_wait(barrier, sub_size)
 
     @pl.when(z == FAR)
     def _():
-        greet_plane(HUB)
-        greet_mates()
-        pl.semaphore_wait(barrier, 2 * mates)
-
-    counts_copy.wait()
+        greet_column(HUB)
+        greet_plane(TOP)
+        pl.semaphore_wait(barrier, sub_size)
 
     def partner(h, step):
         turned = jnp.where(h == 0, step, mates - 1 - step)
@@ -287,14 +294,14 @@
         span = pl.ds(0, chunks * width)
         pltpu.make_async_copy(q_hbm.at[:, span], out_ref.at[:, span], sem).wait()
 
-    def settle_kv(blocks):
+    def settle_kv(blocks, part=0):
         span = pl.ds(0, blocks * PAGE // (2 * per_core))
-        pltpu.make_async_copy(kvbuf.at[:, :, span], kvbuf.at[:, :, span], kv_send.at[0]).wait()
-
-    def kv_block(core, h, held):
+        pltpu.make_async_copy(kvbuf.at[:, :, span], kvbuf.at[:, :, span], kv_send.at[part]).wait()
+
+    def kv_block(core, h, held, skip=0):
         return kv_hbm.at[
             :,
-            pl.ds(0, held * PAGE),
+            pl.ds(skip * PAGE, held * PAGE),
             pl.ds(pl.multiple_of((core * per_core + h) * HD, HD), HD),
         ]
 
@@ -304,34 +311,47 @@
     here = (s + jnp.where(z == TOP, sub_size, 0)) * pages_here
     half = jnp.where(z == TOP, 1, 0)
 
-    def kv_remote(h, core, held, target):
+    def kv_remote(h, core, held, target, recv, part=0, skip=0):
         return pltpu.make_async_remote_copy(
-            src_ref=kv_block(core, h, held),
-            dst_ref=kv_place(h, here, held),
-            send_sem=kv_send.at[0],
-            recv_sem=kv_recv.at[h, half],
+            src_ref=kv_block(core, h, held, skip),
+            dst_ref=kv_place(h, here + skip, held),
+            send_sem=kv_send.at[part],
+            recv_sem=kv_recv.at[h, recv],
             device_id=target,
             device_id_type=MESH,
         )
 
     def kv_await(h, first, count):
         place = kv_place(h, first, count)
-        pltpu.make_async_copy(place, place, kv_recv.at[h, 0 if first < split else 1]).wait()
-
-    def exchange():
+        recv = 0 if first < split else (1 if first == split else 2)
+        pltpu.make_async_copy(place, place, kv_recv.at[h, recv]).wait()
+
+    def own_pages():
         for h in range(per_core):
-            kv_remote(h, 1 - s, pages_here, {"sub": 1 - s}).start()
             pltpu.make_async_copy(
                 kv_block(s, h, pages_here), kv_place(h, here, pages_here), kv_recv.at[h, half]
             ).start()
 
+    def exchange():
+        for h in range(per_core):
+            kv_remote(h, 1 - s, pages_here, {"sub": 1 - s}, half).start()
+
     def hand_far():
         core = sub_size - 1
-        kv_remote(per_core - 1, core, pages_here, {"ctx": FAR, "sub": core}).start()
-
-    def hand_hub(held, h):
+        kv_remote(
+            per_core - 1, core, pages_here, {"ctx": FAR, "sub": core}, 0
+        ).start()
+
+    last = per_core - 1
+
+    def hand_hub(held, h, recv):
         for core in reversed(range(sub_size)):
-            kv_remote(h, core, held, {"ctx": HUB, "sub": core}).start()
+            target = {"ctx": HUB, "sub": core}
+            if core == 0 and h == last and held > 1:
+                kv_remote(h, core, held - 1, target, recv, 1).start()
+                kv_remote(h, core, 1, target, recv, 2, held - 1).start()
+            else:
+                kv_remote(h, core, held, target, recv, 1).start()
 
     def span_of(r):
         first, count = jnp.int32(0), jnp.int32(0)
@@ -411,42 +431,46 @@
     near_pages = range(1, live - 2)
     hub_pages = range(2, live - 1)
     top_pages = range(split, live)
-    last = per_core - 1
-
     def stays_far(step):
         return lax.rem(partner(last, step), sub_size) == sub_size - 1
 
+    def own_queries(h):
+        q_local(h, own_recv.at[h]).start()
+        for step in range(mates):
+            if (step, mates - 1 - step)[h != 0]:
+                q_remote(h, step, z, own_recv.at[h]).start()
+
     @pl.when(z == HUB)
     def _():
         hand_far()
+        own_pages()
+        pl.semaphore_wait(go, 1)
         exchange()
+        own_queries(0)
 
     @pl.when((z == TOP) & (s == 0))
     def _():
         for h in range(per_core):
-            hand_hub(pages_here, h)
+            hand_hub(pages_here, h, 1)
 
     @pl.when((z == TOP) & (s == 1))
     def _():
-        hand_hub(1, 0)
+        hand_hub(1, 0, 2)
 
     @pl.when(z == TOP)
     def _():
+        own_pages()
         exchange()
-
-    @pl.when(z >= HUB)
-    def _():
         for h in range(per_core):
-            q_local(h, own_recv.at[h]).start()
-            for step in range(mates):
-                if (step, mates - 1 - step)[h != 0]:
-                    q_remote(h, step, z, own_recv.at[h]).start()
+            own_queries(h)
 
     @pl.when(z == FAR)
     def _():
         for h in range(per_core):
             recv = q_recv.at[FAR, h, mine]
             for step in range(mates):
+                if h == 0 and step == OWN:
+                    pl.semaphore_wait(go, 1)
                 if h < last:
                     q_remote(h, step, HUB, recv, 0 if step < AHEAD else 1).start()
                 else:
@@ -464,18 +488,20 @@
                             q_local(h, recv).start()
 
         settle(q_send.at[0], AHEAD)
-        pl.semaphore_signal(go, device_id={"ctx": NEAR}, device_id_type=MESH)
+        vouch(NEAR)
 
     @pl.when(z == NEAR)
     def _():
         for step in range(EARLY):
             q_remote(0, step, HUB, q_recv.at[NEAR, 0, mine]).start()
-        pl.semaphore_wait(go, 1)
+        pl.semaphore_wait(go, 2)
         for h in range(per_core):
             for step in range(mates):
                 if h or step >= EARLY:
                     q_remote(h, step, HUB, q_recv.at[NEAR, h, mine]).start()
 
+    counts_copy.wait()
+
     @pl.when((z == HUB) | ((z == FAR) & (s == sub_size - 1)))
     def _():
         span = span_of(FAR)
@@ -489,6 +515,10 @@
             def _():
                 kv_await(h, 0, split)
 
+            @pl.when((n == WHEN) & (z == HUB))
+            def _():
+                own_queries(last)
+
             q_await(FAR, h, partner(h, i))
             turn(FAR, h, i, far_pages, span, FAR, z == FAR)
             return carry
@@ -503,24 +533,57 @@
 
         near_span, hub_span = span_of(NEAR), span_of(HUB)
 
-        def both(n, carry):
+        def near_task(n):
             h, i = n // mates, n % mates
-
-            @pl.when(i == 0)
-            def _():
-                own_await(h)
-                kv_await(h, split, split - 1)
-
             device = partner(h, i)
             q_await(NEAR, h, device)
-            attend(
-                (NEAR, h, device, near_pages, near_span), (HUB, h, device, hub_pages, hub_span)
-            )
-            o_remote(NEAR, h, device, NEAR).start()
-            send_home(HUB, h, device, HUB, alone(h, i))
+            return NEAR, h, device, near_pages, near_span
+
+        def own_task(n):
+            h, i = n // mates, n % mates
+            return HUB, h, partner(h, i), hub_pages, hub_span
+
+        def near_home(n):
+            h, i = n // mates, n % mates
+            o_remote(NEAR, h, partner(h, i), NEAR).start()
+
+        def own_home(n):
+            h, i = n // mates, n % mates
+            send_home(HUB, h, partner(h, i), HUB, alone(h, i))
+
+        def ready(h):
+            own_await(h)
+            kv_await(h, split + pages_here, 1)
+
+        def lead(n, carry):
+            attend(near_task(n))
+            near_home(n)
             return carry
 
-        lax.fori_loop(0, per_core * mates, both, 0)
+        def both(n, carry):
+            ahead = n + jnp.where(n < mates, 0, LAG)
+
+            @pl.when(n == 0)
+            def _():
+                kv_await(0, split, pages_here)
+                ready(0)
+
+            @pl.when(n == mates)
+            def _():
+                kv_await(last, split, pages_here)
+                lax.fori_loop(mates, mates + LAG, lead, 0)
+                ready(last)
+
+            attend(near_task(ahead), own_task(n))
+            near_home(ahead)
+            own_home(n)
+            return carry
+
+        lax.fori_loop(0, per_core * mates - LAG, both, 0)
+        rest = range(per_core * mates - LAG, per_core * mates)
+        attend(*[own_task(n) for n in rest])
+        for n in rest:
+            own_home(n)
 
     @pl.when(z == TOP)
     def _():
@@ -536,13 +599,19 @@
 
             turn(HUB, h, i, top_pages, span, TOP, True)
 
-            @pl.when((s == 1) & (n == LATER))
-            def _():
-                hand_hub(1, last)
-
             return carry
 
         lax.fori_loop(0, per_core * mates, step, 0)
+
+        @pl.when(s == 0)
+        def _():
+            settle_kv(2 * (pages_here * per_core * sub_size - 1), 1)
+            pl.semaphore_signal(go, device_id={"sub": 1}, device_id_type=MESH)
+
+        @pl.when(s == 1)
+        def _():
+            pl.semaphore_wait(go, 1)
+            hand_hub(1, last, 2)
 
     def finals():
         settle(o_recv.at[0], per_core * mates)
@@ -564,13 +633,15 @@
 
     @pl.when(z == TOP)
     def _():
+        settle_kv(2 * pages_here * per_core)
+
         @pl.when(s == 0)
         def _():
-            settle_kv(2 * pages_here * per_core * (1 + sub_size))
+            settle_kv(2, 2)
 
         @pl.when(s == 1)
         def _():
-            settle_kv(2 * per_core * (pages_here + sub_size))
+            settle_kv(2 * per_core * sub_size, 1)
 
     @pl.when(z >= HUB)
     def _():
@@ -625,8 +696,8 @@
             dma((per_core,)),
             dma((slots,)),
             dma((1,)),
-            dma((1,)),
-            dma((per_core, 2)),
+            dma((3,)),
+            dma((per_core, 3)),
             pltpu.SemaphoreType.REGULAR,
         ],
         compiler_params=pltpu.CompilerParams(

time: 31.3 us -> 31.1 us (level)
  no operation moved by 1% of the time
where the time goes in v4:
time: 31.1 us; the launch traced here: 31 us
  Pallas kernels  30.2 us (97%)
  local copies, waits for them, and re-layouts  0.8 us (3%)
    pallas_call x1, Pallas kernels, served(): pl.pallas_call(functools.partial(serve_kernel, (head_size, sub_size, page...  30.2 us
    unnamed x1, local copies, waits for them, and re-layouts  0.8 us

profile of v4, /device:TPU:8, one launch (start us, length us, event | category | flops | bytes accessed | tf_op | source)
XLA Modules:
  0.0 31.0 jit_solution(11180100095864989065)
XLA Ops:
  0.0 30.2 %shard_map.37 = bf16[16,16384]{1,0:T(8,128)(2,1)S(1)} custom-call(s32[4]{0:T(128)} %counts_hbm.1, bf16[16,16384]{1,0:T(8,128)(2,1)} %q_hbm.1, bf16[2,512,512]{2,1,0:T(8,128)(2,1)} %kv_hbm.1), custom_call_target="tpu_custom_call" | custom-call | tf_op jit(solution)/shard_map/pallas_call | solution.py:677
  30.2 0.8 %copy.5 = bf16[16,16384]{1,0:T(8,128)(2,1)} copy(bf16[16,16384]{1,0:T(8,128)(2,1)S(1)} %shard_map.37) | data formatting | bytes 1048576

commit v5 on v4

--- a/solution.py
+++ b/solution.py
@@ -20,7 +20,6 @@
 NEG = -1e30
 MESH = pl.DeviceIdType.MESH
 VMEM_LIMIT = 40000000
-EARLY = 1
 WHEN = 2
 OWN = 2
 LAG = 2
@@ -407,11 +406,14 @@
                 j * tok_rows : (j + 1) * tok_rows, :
             ]
 
-    def attend(*tasks):
+    def attend(*tasks, then=None):
         rooms = (sbuf, tbuf)[: len(tasks)]
         tops = [score(task, room) for task, room in zip(tasks, rooms)]
         for task, room, top in zip(tasks, rooms, tops):
             weigh(task, room, top)
+            if then is not None:
+                then()
+                then = None
 
     def send_home(slot, h, device, plane, stays):
         @pl.when(stays)
@@ -452,10 +454,6 @@
     def _():
         for h in range(per_core):
             hand_hub(pages_here, h, 1)
-
-    @pl.when((z == TOP) & (s == 1))
-    def _():
-        hand_hub(1, 0, 2)
 
     @pl.when(z == TOP)
     def _():
@@ -492,15 +490,50 @@
 
     @pl.when(z == NEAR)
     def _():
-        for step in range(EARLY):
-            q_remote(0, step, HUB, q_recv.at[NEAR, 0, mine]).start()
+        @pl.when(s == 1)
+        def _():
+            q_remote(0, 0, HUB, q_recv.at[NEAR, 0, mine]).start()
+
         pl.semaphore_wait(go, 2)
+
+        @pl.when(s == 0)
+        def _():
+            q_remote(0, 0, HUB, q_recv.at[NEAR, 0, mine]).start()
+
         for h in range(per_core):
             for step in range(mates):
-                if h or step >= EARLY:
+                if h or step:
                     q_remote(h, step, HUB, q_recv.at[NEAR, h, mine]).start()
 
     counts_copy.wait()
+    near_span, hub_span = span_of(NEAR), span_of(HUB)
+
+    def near_task(n):
+        h, i = n // mates, n % mates
+        device = partner(h, i)
+        q_await(NEAR, h, device)
+        return NEAR, h, device, near_pages, near_span
+
+    def own_task(n):
+        h, i = n // mates, n % mates
+        return HUB, h, partner(h, i), hub_pages, hub_span
+
+    def near_home(n):
+        h, i = n // mates, n % mates
+        o_remote(NEAR, h, partner(h, i), NEAR).start()
+
+    def own_home(n):
+        h, i = n // mates, n % mates
+        send_home(HUB, h, partner(h, i), HUB, alone(h, i))
+
+    def ready(h):
+        own_await(h)
+        kv_await(h, split + pages_here, 1)
+
+    def lead(n, carry):
+        attend(near_task(n))
+        near_home(n)
+        return carry
 
     @pl.when((z == HUB) | ((z == FAR) & (s == sub_size - 1)))
     def _():
@@ -519,6 +552,11 @@
             def _():
                 own_queries(last)
 
+            @pl.when((n == mates - 1) & (z == HUB) & (s == 1))
+            def _():
+                kv_await(0, split, pages_here)
+                lead(0, 0)
+
             q_await(FAR, h, partner(h, i))
             turn(FAR, h, i, far_pages, span, FAR, z == FAR)
             return carry
@@ -531,51 +569,27 @@
         def _():
             kv_await(last, 0, split)
 
-        near_span, hub_span = span_of(NEAR), span_of(HUB)
-
-        def near_task(n):
-            h, i = n // mates, n % mates
-            device = partner(h, i)
-            q_await(NEAR, h, device)
-            return NEAR, h, device, near_pages, near_span
-
-        def own_task(n):
-            h, i = n // mates, n % mates
-            return HUB, h, partner(h, i), hub_pages, hub_span
-
-        def near_home(n):
-            h, i = n // mates, n % mates
-            o_remote(NEAR, h, partner(h, i), NEAR).start()
-
-        def own_home(n):
-            h, i = n // mates, n % mates
-            send_home(HUB, h, partner(h, i), HUB, alone(h, i))
-
-        def ready(h):
-            own_await(h)
-            kv_await(h, split + pages_here, 1)
-
-        def lead(n, carry):
-            attend(near_task(n))
-            near_home(n)
-            return carry
-
         def both(n, carry):
-            ahead = n + jnp.where(n < mates, 0, LAG)
+            ahead = n + jnp.where(n < mates, s, LAG)
+
+            @pl.when((n == 0) & (s == 0))
+            def _():
+                kv_await(0, split, pages_here)
 
             @pl.when(n == 0)
             def _():
-                kv_await(0, split, pages_here)
                 ready(0)
 
+            @pl.when(n == mates - s)
+            def _():
+                kv_await(last, split, pages_here)
+
             @pl.when(n == mates)
             def _():
-                kv_await(last, split, pages_here)
-                lax.fori_loop(mates, mates + LAG, lead, 0)
+                lax.fori_loop(mates + s, mates + LAG, lead, 0)
                 ready(last)
 
-            attend(near_task(ahead), own_task(n))
-            near_home(ahead)
+            attend(near_task(ahead), own_task(n), then=lambda: near_home(ahead))
             own_home(n)
             return carry
 
@@ -596,6 +610,10 @@
             def _():
                 own_await(h)
                 kv_await(h, split, split)
+
+            @pl.when((n == 0) & (s == 1))
+            def _():
+                hand_hub(1, 0, 2)
 
             turn(HUB, h, i, top_pages, span, TOP, True)
 

time: 31.1 us -> 30.8 us (level)
  Pallas kernels: 30.2 us -> 29.8 us
    pallas_call x1, Pallas kernels: 30.2 us -> 29.8 us  [served(): pl.pallas_call(functools.partial(serve_kernel, (head_size, sub_size, page...]
where the time goes in v5:
time: 30.8 us; the launch traced here: 30.6 us
  Pallas kernels  29.8 us (97%)
  local copies, waits for them, and re-layouts  0.8 us (3%)
    pallas_call x1, Pallas kernels, served(): pl.pallas_call(functools.partial(serve_kernel, (head_size, sub_size, page...  29.8 us
    unnamed x1, local copies, waits for them, and re-layouts  0.8 us

profile of v5, /device:TPU:8, one launch (start us, length us, event | category | flops | bytes accessed | tf_op | source)
XLA Modules:
  0.0 30.6 jit_solution(6989295534028749800)
XLA Ops:
  0.0 29.8 %shard_map.37 = bf16[16,16384]{1,0:T(8,128)(2,1)S(1)} custom-call(s32[4]{0:T(128)} %counts_hbm.1, bf16[16,16384]{1,0:T(8,128)(2,1)} %q_hbm.1, bf16[2,512,512]{2,1,0:T(8,128)(2,1)} %kv_hbm.1), custom_call_target="tpu_custom_call" | custom-call | tf_op jit(solution)/shard_map/pallas_call | solution.py:695
  29.8 0.8 %copy.5 = bf16[16,16384]{1,0:T(8,128)(2,1)} copy(bf16[16,16384]{1,0:T(8,128)(2,1)S(1)} %shard_map.37) | data formatting | bytes 1048576

commit v6 on v5

--- a/solution.py
+++ b/solution.py
@@ -217,8 +217,8 @@
 
     @pl.when(z == HUB)
     def _():
+        greet_column(FAR)
         greet_column(NEAR)
-        greet_column(FAR)
         greet_plane(TOP)
         pl.semaphore_wait(barrier, sub_size)
 

time: 30.8 us -> 30.8 us (level)
  no operation moved by 1% of the time
where the time goes in v6:
time: 30.8 us; the launch traced here: 30.6 us
  Pallas kernels  29.8 us (97%)
  local copies, waits for them, and re-layouts  0.8 us (3%)
    pallas_call x1, Pallas kernels, served(): pl.pallas_call(functools.partial(serve_kernel, (head_size, sub_size, page...  29.8 us
    unnamed x1, local copies, waits for them, and re-layouts  0.8 us

profile of v6, /device:TPU:8, one launch (start us, length us, event | category | flops | bytes accessed | tf_op | source)
XLA Modules:
  0.0 30.6 jit_solution(12144926106915534106)
XLA Ops:
  0.0 29.8 %shard_map.37 = bf16[16,16384]{1,0:T(8,128)(2,1)S(1)} custom-call(s32[4]{0:T(128)} %counts_hbm.1, bf16[16,16384]{1,0:T(8,128)(2,1)} %q_hbm.1, bf16[2,512,512]{2,1,0:T(8,128)(2,1)} %kv_hbm.1), custom_call_target="tpu_custom_call" | custom-call | tf_op jit(solution)/shard_map/pallas_call | solution.py:695
  29.8 0.8 %copy.5 = bf16[16,16384]{1,0:T(8,128)(2,1)} copy(bf16[16,16384]{1,0:T(8,128)(2,1)S(1)} %shard_map.37) | data formatting | bytes 1048576
